TPU v7x, 32 devices: a whole 2x2x4 slice. The times are simulated.
32 devices in a mesh: orb: 4 (over y, x), grid: 8 (over z, core).
Axes of the slice: x: 2, y: 2, z: 4, core: 2. Of those that a mesh axis runs over, the one named last changes fastest.
Arguments:
- orbitals: float32 [32, 2048, 128], P('orb', 'grid'), may hold values from -6 to 6
- previous: float32 [32, 2048, 128], P('orb', 'grid'), may hold values from -6 to 6
- potential: float32 [32, 2048, 128], P('orb', 'grid'), may hold values from -3 to 3
- partners: int32 [32, 3], P(('orb', 'grid')), may hold values from 0 to 31, as said below
- offsets: int32 [32, 3, 3], P(('orb', 'grid')), may hold values from -16 to 16, as said below
Outputs:
- advanced: float32 [32, 2048, 128], P('orb', 'grid')
- exchange_force: float32 [32, 2048, 128], P('orb', 'grid')
Inputs may be any that keep to these rules, and one draw needn't show every extreme that they name: `partners`: row n names three different orbitals among n + 1 to n + 4, counted modulo 32; so every intersecting pair is listed once, by its first orbital. There are integer box corners of the orbitals with offsets[n, q, :] = corner[partners[n, q]] - corner[n]; both ends of the range occur in every draw.
All inputs are finite; a program needn't handle non-finite values.
Results may differ from a plain program's by a relative error of at most 0.0003.
Values sent between devices are 32-bit elements; how exact they have to be, the bound alone decides.
A program may use at most 128 MiB of HBM per device.

v0:
```python
import math

import jax
import jax.numpy as jnp
from jax import lax
from jax.sharding import PartitionSpec as P

B = 64
SWEEPS = 4
AHEAD = 4


coulomb_factor = 4.0 * math.pi
exact_share = 0.25
verlet_factor = 0.05
lower_edge = 0.5
upper_edge = 16.0


def from_behind(array, axis, by):
    count = lax.axis_size(axis)
    return lax.ppermute(array, axis, [(i, (i + by) % count) for i in range(count)])


def apply_operator(grid_field):
    leading = grid_field.ndim - 3
    padded = jnp.pad(grid_field, [(0, 0)] * leading + [(2, 2)] * 3)
    extent = grid_field.shape[-1]

    def displaced(axis_number, offset_cells):
        corner = [2, 2, 2]
        corner[axis_number] = 2 + offset_cells
        return padded[
            ...,
            corner[0] : corner[0] + extent,
            corner[1] : corner[1] + extent,
            corner[2] : corner[2] + extent,
        ]

    nearest = (
        displaced(0, 1)
        + displaced(0, -1)
        + displaced(1, 1)
        + displaced(1, -1)
        + displaced(2, 1)
        + displaced(2, -1)
    )
    farther = (
        displaced(0, 2)
        + displaced(0, -2)
        + displaced(1, 2)
        + displaced(1, -2)
        + displaced(2, 2)
        + displaced(2, -2)
    )
    return 7.5 * grid_field - 4.0 / 3.0 * nearest + 1.0 / 12.0 * farther


def sweep_weights():
    centre = 0.5 * (upper_edge + lower_edge)
    radius = 0.5 * (upper_edge - lower_edge)
    ratio_sigma = centre / radius
    previous_rho = 1.0 / ratio_sigma
    weights = []
    for turn_index in range(SWEEPS - 1):
        current_rho = 1.0 / (2.0 * ratio_sigma - previous_rho)
        weights.append((current_rho * previous_rho, 2.0 * current_rho / radius))
        previous_rho = current_rho
    return (centre, weights)


def solve_potential(density):
    centre, weights = sweep_weights()
    residual = coulomb_factor * density
    direction = residual / centre
    solution = jnp.zeros_like(density)
    for turn_index in range(SWEEPS):
        solution = solution + direction
        residual = residual - apply_operator(direction)
        if turn_index + 1 < SWEEPS:
            keep_weight, residual_weight = weights[turn_index]
            direction = keep_weight * direction + residual_weight * residual
    return solution


def shift_box(one_box, offset, direction_sign):
    extent = one_box.shape[0]
    reach_cells = extent // 4
    padded = jnp.pad(one_box, reach_cells)
    corner = (reach_cells + direction_sign * offset).astype(jnp.int32)
    return lax.dynamic_slice(padded, (corner[0], corner[1], corner[2]), (extent, extent, extent))


def pair_terms(own_box, partner_boxes, pair_offsets):

    def single(partner_box, offset):
        moved_box = shift_box(partner_box, offset, 1)
        potential_box = solve_potential(own_box * moved_box)
        return (potential_box * moved_box, shift_box(potential_box * own_box, offset, -1))

    own_terms, partner_terms = jax.vmap(single)(partner_boxes, pair_offsets)
    return (jnp.sum(own_terms, axis=0), partner_terms)


def build_windows(orbitals, upper_rows, count_local, steps_ahead):
    slab_count = lax.axis_size("grid")
    tail_shape = orbitals.shape[1:]
    blocks = jnp.concatenate([orbitals, upper_rows], axis=0)
    blocks = blocks.reshape((slab_count + steps_ahead, count_local) + tail_shape)
    ahead_rows = jnp.concatenate(
        [blocks[distance + 1 : distance + 1 + slab_count] for distance in range(steps_ahead)],
        axis=1,
    )
    windows = jnp.concatenate([blocks[:slab_count], ahead_rows], axis=1)
    return windows.reshape((slab_count * (count_local + AHEAD),) + tail_shape)


def fold_windows(returned, count_local, steps_ahead):
    slab_count = lax.axis_size("grid")
    tail_shape = returned.shape[1:]
    blocks = returned.reshape((slab_count, count_local + AHEAD) + tail_shape)
    ahead_rows = blocks[:, count_local:]
    summed = jnp.pad(blocks[:, :count_local], ((0, steps_ahead), (0, 0), (0, 0), (0, 0)))
    for distance in range(steps_ahead):
        ahead_part = ahead_rows[:, distance * count_local : (distance + 1) * count_local]
        summed = summed + jnp.pad(
            ahead_part, ((distance + 1, steps_ahead - distance - 1), (0, 0), (0, 0), (0, 0))
        )
    flattened = summed.reshape(((slab_count + steps_ahead) * count_local,) + tail_shape)
    kept_rows = slab_count * count_local
    spilled = from_behind(flattened[kept_rows : kept_rows + AHEAD], "orb", 1)
    return flattened[:kept_rows] + jnp.pad(spilled, ((0, kept_rows - AHEAD), (0, 0), (0, 0)))


def local(orbitals, previous, potential, partners, offsets):
    count_local = partners.shape[0]
    width_last = orbitals.shape[2]
    total_orbitals = lax.axis_size(("orb", "grid")) * count_local
    steps_ahead = -(-AHEAD // count_local)
    upper_rows = from_behind(orbitals[:AHEAD], "orb", -1)
    windows = build_windows(orbitals, upper_rows, count_local, steps_ahead)
    widened = lax.all_to_all(windows, "grid", split_axis=0, concat_axis=1, tiled=True)
    full_rows = widened.shape[1]
    extended = widened.reshape(count_local + AHEAD, B, B, B)
    own_boxes = extended[:count_local]
    first_index = lax.axis_index(("orb", "grid")) * count_local
    local_index = jnp.remainder(partners - first_index, total_orbitals)

    def per_orbital(packed):
        own_box, chosen, pair_offsets = packed
        return pair_terms(own_box, extended[chosen], pair_offsets)

    own_force, partner_force = lax.map(per_orbital, (own_boxes, local_index, offsets))
    spread = (
        jnp.zeros_like(extended)
        .at[local_index.reshape(-1)]
        .add(partner_force.reshape((-1,) + extended.shape[1:]))
    )
    kinetic = (-0.5 * apply_operator(own_boxes)).reshape(count_local, full_rows, width_last)
    all_force = jnp.concatenate([own_force + spread[:count_local], spread[count_local:]], axis=0)
    packed_all = (exact_share * all_force).reshape(count_local + AHEAD, full_rows, width_last)
    returned, restored = (
        lax.all_to_all(packed_all, "grid", split_axis=1, concat_axis=0, tiled=True),
        lax.all_to_all(kinetic, "grid", split_axis=1, concat_axis=0, tiled=True),
    )
    exchange_force = fold_windows(returned, count_local, steps_ahead)
    advanced = (
        2.0 * orbitals
        - previous
        + verlet_factor * (restored + exchange_force - potential * orbitals)
    )
    return (advanced, exchange_force)


def solution(mesh):
    in_specs = (
        P("orb", "grid", None),
        P("orb", "grid", None),
        P("orb", "grid", None),
        P(("orb", "grid"), None),
        P(("orb", "grid"), None, None),
    )
    out_specs = (P("orb", "grid", None), P("orb", "grid", None))
    return jax.shard_map(local, mesh=mesh, in_specs=in_specs, out_specs=out_specs, check_vma=False)
```

profile of v0, /device:TPU:16, one launch (start us, length us, event | category | flops | bytes accessed | tf_op | source)
XLA Modules:
  0.0 633.2 jit_solution(1939812428147759683)
XLA Ops:
  0.6 1.1 slice.280
  1.7 2.5 collective-permute-start
  4.2 1.3 constant_dynamic-update-slice_fusion.1
  5.5 1.3 bitcast_dynamic-update-slice_fusion
  6.8 8.6 %collective-permute-done = f32[4,256,128]{2,1,0:T(8,128)S(1)} collective-permute-done((f32[4,256,128]{2,1,0:T(8,128)S(1)}, f32[4,256,128]{2,1,0:T(8,128)S(1)}, u32[]{:S(2)}, u32[]{:S(2)}) %collective-permute-start) | collective-permute-done | bytes 524320 | tf_op jit(solution)/shard_map/ppermute | solution.py:22
  15.8 2.4 copy-done.2
  18.2 5.2 all-to-all-start
  23.8 112.7 %all-to-all-done = f32[40,256,128]{2,1,0:T(8,128)} async-done(((f32[40,256,128]{2,1,0:T(8,128)}), f32[40,256,128]{2,1,0:T(8,128)}, u32[]{:S(2)}, u32[]{:S(2)}) %all-to-all-start) | async-done | bytes 5242912 | tf_op jit(solution)/shard_map/all_to_all | solution.py:142
  136.6 5.5 copy.54
  142.0 1.3 slice.398
  143.3 8.5 %reshape.85 = f32[5,64,64,64]{3,2,1,0:T(8,128)} reshape(f32[5,8,256,128]{3,2,1,0:T(8,128)} %copy.54) | data formatting | bytes 10485760 | tf_op jit(solution)/shard_map/reshape | solution.py:144
  151.8 7.5 %gather_fusion = f32[3,64,64,64]{3,2,1,0:T(8,128)} fusion(f32[5,64,64,64]{3,2,1,0:T(8,128)} %reshape.85, s32[1024]{0:T(1024)S(1)} %pad_clamp_fusion), kind=kCustom, calls=%fused_computation | custom fusion | bytes 6291468 | tf_op jit(solution)/shard_map/while/body/eval_jaxpr/gather | solution.py:151
  159.3 10.5 %pad.51 = f32[3,96,96,96]{3,2,1,0:T(8,128)} pad(f32[3,64,64,64]{3,2,1,0:T(8,128)} %gather_fusion, f32[]{:T(128)} %constant.45.clone.1), padding=0_0x16_16x16_16x16_16 | pad | bytes 13762564 | tf_op jit(solution)/shard_map/while/body/eval_jaxpr/vmap(jit(_pad))/pad | solution.py:89
  169.8 3.5 broadcast.154.clone
  173.3 20.9 %while.2 = (s32[]{:T(128)}, f32[3,96,96,96]{3,2,1,0:T(8,128)}, s32[3,4]{1,0:T(4,128)S(1)}, f32[3,64,64,64]{3,2,1,0:T(8,128)}, s32[]{:T(128)}) while((s32[]{:T(128)}, f32[3,96,96,96]{3,2,1,0:T(8,128)}, s32[3,4]{1,0:T(4,128)S(1)}, f32[3,64,64,64]{3,2,1,0:T(8,128)}, s32[]{:T(128)}) %tuple.70), condition=%wide.while_cond, body=%wide.while_body.sunk | while | flops 2 | bytes 4196993 | solution.py:91
  174.0 6.3 dynamic-slice_dynamic-update-slice_fusion.4
  180.3 0.7 fusion.84
  181.0 6.3 dynamic-slice_dynamic-update-slice_fusion.4
  187.3 0.7 fusion.84
  187.9 6.3 dynamic-slice_dynamic-update-slice_fusion.4
  194.5 6.9 %multiply_multiply_fusion = f32[3,64,64,64]{3,2,1,0:T(8,128)} fusion(f32[3,64,64,64]{3,2,1,0:T(8,128)} %get-tuple-element.30, f32[64,64,64]{2,1,0:T(8,128)S(1)} %mul.165), kind=kLoop, calls=%fused_computation.93 | loop fusion | flops 1572864 | bytes 7340032 | tf_op jit(solution)/shard_map/while/body/eval_jaxpr/vmap()/div | solution.py:75
  201.4 36.1 %multiply_add_fusion.1 = (f32[3,64,64,64]{3,2,1,0:T(8,128)}, f32[3,64,64,64]{3,2,1,0:T(8,128)}) fusion(f32[3,64,64,64]{3,2,1,0:T(8,128)} %get-tuple-element.30, f32[64,64,64]{2,1,0:T(8,128)S(1)} %mul.165, f32[3,64,64,64]{3,2,1,0:T(8,128)} %multiply_multiply_fusion), kind=kLoop, calls=%fused_computation.92 | loop fusion | flops 16515072 | bytes 13631488 | tf_op jit(solution)/shard_map/while/body/eval_jaxpr/vmap()/add | solution.py:82
  237.5 35.9 %multiply_add_fusion = (f32[3,64,64,64]{3,2,1,0:T(8,128)}, f32[3,64,64,64]{3,2,1,0:T(8,128)}) fusion(f32[3,64,64,64]{3,2,1,0:T(8,128)} %get-tuple-element.101, f32[3,64,64,64]{3,2,1,0:T(8,128)} %get-tuple-element.102), kind=kLoop, calls=%fused_computation.91 | loop fusion | flops 14942208 | bytes 12582912 | tf_op jit(solution)/shard_map/while/body/eval_jaxpr/vmap()/add | solution.py:82
  273.5 43.8 %multiply_reduce_fusion = (f32[64,64,64]{2,1,0:T(8,128)}, f32[3,64,64,64]{3,2,1,0:T(8,128)}) fusion(f32[3,64,64,64]{3,2,1,0:T(8,128)} %get-tuple-element.30, f32[3,64,64,64]{3,2,1,0:T(8,128)} %get-tuple-element.100, f32[3,64,64,64]{3,2,1,0:T(8,128)} %get-tuple-element.99, f32[3,64,64,64]{3,2,1,0:T(8,128)} %get-tuple-element.101, f32[64,64,64]{2,1,0:T(8,128)S(1)} %mul.165), kind=kLoop, calls=%fused_computation.90 | loop fusion | flops 20185088 | bytes 17825792 | tf_op jit(solution)/shard_map/while/body/eval_jaxpr/reduce_sum | solution.py:102
  317.2 6.9 %broadcast_multiply_fusion = f32[3,64,64,64]{3,2,1,0:T(8,128)} fusion(f32[3,64,64,64]{3,2,1,0:T(8,128)} %get-tuple-element.98, f32[64,64,64]{2,1,0:T(8,128)S(1)} %mul.165), kind=kLoop, calls=%fused_computation.96 | loop fusion | flops 786432 | bytes 7340032 | tf_op jit(solution)/shard_map/while/body/eval_jaxpr/vmap()/mul | solution.py:99
  324.1 10.5 %pad.55 = f32[3,96,96,96]{3,2,1,0:T(8,128)} pad(f32[3,64,64,64]{3,2,1,0:T(8,128)} %broadcast_multiply_fusion, f32[]{:T(128)} %constant.45.clone.1), padding=0_0x16_16x16_16x16_16 | pad | bytes 13762564 | tf_op jit(solution)/shard_map/while/body/eval_jaxpr/vmap(jit(_pad))/pad | solution.py:89
  334.6 3.4 broadcast.154
  338.0 20.1 %while.3 = (s32[]{:T(128)}, f32[3,96,96,96]{3,2,1,0:T(8,128)}, s32[3,4]{1,0:T(4,128)S(1)}, f32[3,64,64,64]{3,2,1,0:T(8,128)}, s32[]{:T(128)}) while((s32[]{:T(128)}, f32[3,96,96,96]{3,2,1,0:T(8,128)}, s32[3,4]{1,0:T(4,128)S(1)}, f32[3,64,64,64]{3,2,1,0:T(8,128)}, s32[]{:T(128)}) %tuple.73), condition=%wide.while_cond.1, body=%wide.while_body.1.sunk | while | flops 2 | bytes 4196993 | solution.py:91
  338.6 6.1 dynamic-slice_dynamic-update-slice_fusion.5
  345.3 6.1 dynamic-slice_dynamic-update-slice_fusion.5
  352.0 6.1 dynamic-slice_dynamic-update-slice_fusion.5
  358.1 5.3 broadcast_in_dim.31
  363.4 11.9 %scatter_fusion = f32[5,64,64,64]{3,2,1,0:T(8,128)} fusion(f32[5,64,64,64]{3,2,1,0:T(8,128)} %broadcast_in_dim.31, s32[3]{0:T(128)S(1)} %fusion.74, f32[3,64,64,64]{3,2,1,0:T(8,128)} %get-tuple-element.38), kind=kCustom, calls=%fused_computation.1 | custom fusion | flops 786432 | bytes 9437196 | tf_op jit(solution)/shard_map/scatter-add | solution.py:157
  375.3 8.5 %slice.400 = f32[4,64,64,64]{3,2,1,0:T(8,128)} slice(f32[5,64,64,64]{3,2,1,0:T(8,128)} %scatter_fusion), slice={[1:5], [0:64], [0:64], [0:64]} | slice | bytes 8388608 | tf_op jit(solution)/shard_map/slice | solution.py:160
  383.9 2.0 slice_add_fusion
  385.8 1.3 concatenate.26
  387.2 7.3 %concatenate.27 = f32[4,2048,128]{2,1,0:T(8,128)} reshape(f32[4,64,64,64]{3,2,1,0:T(8,128)} %slice.400) | data formatting | bytes 8388608 | tf_op jit(solution)/shard_map/concatenate | solution.py:160
  394.5 2.5 maximum_multiply_fusion
  397.0 13.0 %copy.63 = f32[5,2048,128]{2,0,1:T(8,128)} copy(f32[5,2048,128]{2,1,0:T(8,128)S(1)} %maximum_multiply_fusion) | data formatting | bytes 10485760 | tf_op jit(solution)/shard_map/mul | solution.py:161
  410.0 8.2 %all-to-all-start.2 = ((f32[5,2048,128]{2,0,1:T(8,128)}), f32[5,2048,128]{2,0,1:T(8,128)}, u32[]{:S(2)}, u32[]{:S(2)}) async-start(f32[5,2048,128]{2,0,1:T(8,128)} %copy.63), calls=%async_computation.2 | async-start | bytes 16777216 | tf_op jit(solution)/shard_map/all_to_all | solution.py:163
  418.5 4.0 fusion.56
  422.5 3.4 reshape.84
  425.9 172.9 %all-to-all-done.2 = f32[5,2048,128]{2,0,1:T(8,128)} async-done(((f32[5,2048,128]{2,0,1:T(8,128)}), f32[5,2048,128]{2,0,1:T(8,128)}, u32[]{:S(2)}, u32[]{:S(2)}) %all-to-all-start.2) | async-done | bytes 5242912 | tf_op jit(solution)/shard_map/all_to_all | solution.py:163
  598.8 7.5 %all-to-all-start.1 = ((f32[1,2048,128]{2,0,1:T(1,128)}), f32[1,2048,128]{2,0,1:T(1,128)}, u32[]{:S(2)}, u32[]{:S(2)}) async-start(f32[1,2048,128]{2,0,1:T(1,128)} %reshape.84), calls=%async_computation.1 | async-start | bytes 2097152 | tf_op jit(solution)/shard_map/all_to_all | solution.py:164
  606.3 4.4 copy.68
  611.2 2.5 collective-permute-start.1
  613.9 15.7 %all-to-all-done.1 = f32[1,2048,128]{2,0,1:T(1,128)} async-done(((f32[1,2048,128]{2,0,1:T(1,128)}), f32[1,2048,128]{2,0,1:T(1,128)}, u32[]{:S(2)}, u32[]{:S(2)}) %all-to-all-start.1) | async-done | bytes 1048608 | tf_op jit(solution)/shard_map/all_to_all | solution.py:164
  629.6 3.6 multiply_add_fusion.2
  (42 shorter events, 4.7 us)
Async XLA Ops:
  1.7 13.7 %collective-permute-start = (f32[4,256,128]{2,1,0:T(8,128)S(1)}, f32[4,256,128]{2,1,0:T(8,128)S(1)}, u32[]{:S(2)}, u32[]{:S(2)}) collective-permute-start(f32[4,256,128]{2,1,0:T(8,128)S(1)} %slice.280), channel_id=1, source_target_pairs={{0,24},{8,0},{16,8},{24,16},{1,25},{9,1},{17,9},{25,17},{2,26},{10... | collective-permute-start | bytes 1572872 | tf_op jit(solution)/shard_map/ppermute | solution.py:22
  15.7 7.7 %copy-start.4 = (s32[1,3,3]{2,0,1:T(1,128)S(1)}, s32[1,3,3]{2,0,1:T(1,128)}, u32[]{:S(2)}) copy-start(s32[1,3,3]{2,0,1:T(1,128)} %param.9) | copy-start | bytes 112
  15.7 8.1 %copy-start.5 = (s32[1,3]{1,0:T(1,128)S(1)}, s32[1,3]{1,0:T(1,128)}, u32[]{:S(2)}) copy-start(s32[1,3]{1,0:T(1,128)} %param.8) | copy-start | bytes 40
  15.8 2.4 copy-start.2
  18.2 118.4 %all-to-all-start = ((f32[40,256,128]{2,1,0:T(8,128)}), f32[40,256,128]{2,1,0:T(8,128)}, u32[]{:S(2)}, u32[]{:S(2)}) async-start(f32[40,256,128]{2,1,0:T(8,128)} %bitcast.93), calls=%async_computation | async-start | bytes 10485760 | tf_op jit(solution)/shard_map/all_to_all | solution.py:142
  375.3 8.5 %copy-start.1 = (f32[64,64,64]{2,1,0:T(8,128)S(1)}, f32[64,64,64]{2,1,0:T(8,128)}, u32[]{:S(2)}) copy-start(f32[64,64,64]{2,1,0:T(8,128)} %get-tuple-element.97) | copy-start | bytes 3145732
  387.2 7.3 %copy-start.3 = (f32[1,2048,128]{2,1,0:T(8,128)S(1)}, f32[1,2048,128]{2,1,0:T(8,128)}, u32[]{:S(2)}) copy-start(f32[1,2048,128]{2,1,0:T(8,128)} %concatenate.26) | copy-start | bytes 3145732
  410.0 188.8 %all-to-all-start.2 = ((f32[5,2048,128]{2,0,1:T(8,128)}), f32[5,2048,128]{2,0,1:T(8,128)}, u32[]{:S(2)}, u32[]{:S(2)}) async-start(f32[5,2048,128]{2,0,1:T(8,128)} %copy.63), calls=%async_computation.2 | async-start | bytes 16777216 | tf_op jit(solution)/shard_map/all_to_all | solution.py:163
  598.8 30.8 %all-to-all-start.1 = ((f32[1,2048,128]{2,0,1:T(1,128)}), f32[1,2048,128]{2,0,1:T(1,128)}, u32[]{:S(2)}, u32[]{:S(2)}) async-start(f32[1,2048,128]{2,0,1:T(1,128)} %reshape.84), calls=%async_computation.1 | async-start | bytes 2097152 | tf_op jit(solution)/shard_map/all_to_all | solution.py:164
  611.1 18.5 %copy-start = (f32[8,256,128]{2,1,0:T(8,128)S(1)}, f32[8,256,128]{2,1,0:T(8,128)}, u32[]{:S(2)}) copy-start(f32[8,256,128]{2,1,0:T(8,128)} %param.5) | copy-start | bytes 3145732
  611.2 18.4 %collective-permute-start.1 = (f32[4,256,128]{2,1,0:T(8,128)S(1)}, f32[4,256,128]{2,1,0:T(8,128)}, u32[]{:S(2)}, u32[]{:S(2)}) collective-permute-start(f32[4,256,128]{2,1,0:T(8,128)S(1)} %add_bitcast_fusion), channel_id=1, source_target_pairs={{0,8},{8,16},{16,24},{24,0},{1,9},{9,17},{17,25},{25,1},{2,10},{10... | collective-permute-start | bytes 1572872 | tf_op jit(solution)/shard_map/ppermute | solution.py:22
where the time goes:
time: 639 us; the launch traced here: 633 us
  waiting for transfers between devices  310 us (49%)
  other arithmetic  154 us (24%)
  local copies, waits for them, and re-layouts  143 us (22%)
  starting transfers between devices  25.9 us (4%)
    all_to_all x1, waiting for transfers between devices, local(): lax.all_to_all(packed_all, 'grid', split_axis=1, concat_axis=0, tiled=True)  173 us
    all_to_all x1, waiting for transfers between devices, local(): lax.all_to_all(windows, 'grid', split_axis=0, concat_axis=1, tiled=True)  113 us
    add x2, other arithmetic, solve_potential(): direction = keep_weight * direction + residual_weight * residual  72 us
    reduce_sum x1, other arithmetic, pair_terms(): return (jnp.sum(own_terms, axis=0), partner_terms)  43.8 us
    gather x18, local copies, waits for them, and re-layouts  40.9 us
    pad x2, local copies, waits for them, and re-layouts, shift_box(): padded = jnp.pad(one_box, reach_cells)  21 us
    all_to_all x1, waiting for transfers between devices, local(): lax.all_to_all(kinetic, 'grid', split_axis=1, concat_axis=0, tiled=True)  15.7 us
    mul x1, local copies, waits for them, and re-layouts, local(): exact_share * all_force  13 us
  transfers between devices with their start and end apart: 5, of which 4 were waited for; matrix products, arithmetic and copies ran while one was open for 2% of the time, Pallas kernels for 0%

commit v1 on v0

v1 whole, which is shorter than its diff:
```python
import functools
import math

import jax
import jax.numpy as jnp
from jax import lax
from jax.experimental import pallas as pl
from jax.experimental.pallas import tpu as pltpu
from jax.sharding import PartitionSpec as P

B = 64
SWEEPS = 4
AHEAD = 4
SHIFT = 16
CORES = 2
LANES = 2 * B
PLANE_ROWS = B // 2
CHUNK = 4
ROW_PAD = SHIFT // 2
PADDED_ROWS = PLANE_ROWS + 3 * ROW_PAD

coulomb_factor = 4.0 * math.pi
exact_share = 0.25
verlet_factor = 0.05
lower_edge = 0.5
upper_edge = 16.0


def sweep_weights():
    centre = 0.5 * (upper_edge + lower_edge)
    radius = 0.5 * (upper_edge - lower_edge)
    ratio_sigma = centre / radius
    previous_rho = 1.0 / ratio_sigma
    weights = []
    for turn_index in range(SWEEPS - 1):
        current_rho = 1.0 / (2.0 * ratio_sigma - previous_rho)
        weights.append((current_rho * previous_rho, 2.0 * current_rho / radius))
        previous_rho = current_rho
    return (centre, weights)


def two_parts(x):
    high = x.astype(jnp.bfloat16)
    low = (x - high.astype(jnp.float32)).astype(jnp.bfloat16)
    return [high, low]


def stencil_matrix():
    source = lax.broadcasted_iota(jnp.int32, (2 * LANES, 2 * LANES), 0) % LANES
    column = lax.broadcasted_iota(jnp.int32, (2 * LANES, 2 * LANES), 1)
    target = column % LANES
    gap = jnp.abs(source - target)
    same = (source // B) == (target // B)
    inside = jnp.where(
        same,
        jnp.where(gap == 0, 90.0, jnp.where(gap == 1, -16.0, jnp.where(gap == 2, 1.0, 0.0))),
        jnp.where(gap == B, -16.0, 0.0),
    )
    across = jnp.where(gap == B, -16.0, 0.0)
    return jnp.where(column < LANES, inside, across).astype(jnp.bfloat16)


def operator12(window, matrix, count):
    rows = count * PLANE_ROWS

    def planes(start):
        return window[start : start + count].reshape(rows, LANES)

    x = planes(2)
    product = jnp.dot(
        jnp.concatenate(two_parts(x), axis=1), matrix, preferred_element_type=jnp.float32
    )
    inside, across = product[:, :LANES], product[:, LANES:]
    lane = lax.broadcasted_iota(jnp.int32, (rows, LANES), 1)
    row = lax.broadcasted_iota(jnp.int32, (rows, LANES), 0) % PLANE_ROWS
    downward = x + jnp.where(lane < B, across, 0.0)
    upward = x + jnp.where(lane >= B, across, 0.0)
    downward = jnp.where(row == 0, 0.0, pltpu.roll(downward, 1, 0))
    upward = jnp.where(row == PLANE_ROWS - 1, 0.0, pltpu.roll(upward, rows - 1, 0))
    beside = planes(0) + planes(4) - 16.0 * (planes(1) + planes(3))
    return inside + downward + upward + beside


def shift_matrix(odd, across):
    shape = (LANES, LANES)
    source = lax.broadcasted_iota(jnp.int32, shape, 0)
    target = lax.broadcasted_iota(jnp.int32, shape, 1)
    cells = (source % B) == (target % B) + across
    half = target // B + odd - source // B

    def one(wanted):
        return jnp.where(cells & (half == wanted), 1.0, 0.0).astype(jnp.bfloat16)

    here, following = one(0), one(2)
    return jnp.concatenate([here, here, following, following], axis=0)


def shifted(padded, first, offset, matrix):
    plane = SHIFT + first + offset[0]
    row = ROW_PAD + (offset[1] >> 1)
    rows = CHUNK * PLANE_ROWS
    here = padded[pl.ds(plane, CHUNK), pl.ds(row, PLANE_ROWS), :].reshape(rows, LANES)
    following = padded[pl.ds(plane, CHUNK), pl.ds(row + 1, PLANE_ROWS), :].reshape(rows, LANES)
    parts = jnp.concatenate(two_parts(here) + two_parts(following), axis=1)
    return jnp.dot(parts, matrix, preferred_element_type=jnp.float32)


def pair_kernel(
    chosen, offsets, mine, theirs, kept, passed,
    padded, own, moved, first, second, residual, total, own_force, stencil, mover,
):
    chips, _, depth = mine.shape[:3]
    core = lax.rem(lax.axis_index("grid"), CORES)
    chunks = B // CHUNK
    centre, weights = sweep_weights()
    shape3 = (CHUNK, PLANE_ROWS, LANES)

    stencil[...] = stencil_matrix()
    zero_plane = jnp.zeros((2, PLANE_ROWS, LANES), jnp.float32)
    for buffer in (first, second):
        buffer[0:2] = zero_plane
        buffer[B + 2 : B + 4] = zero_plane
    own_force[...] = jnp.zeros_like(own_force)
    kept[...] = jnp.zeros_like(kept)
    passed[...] = jnp.zeros_like(passed)

    @pl.loop(0, padded.shape[0])
    def _(plane):
        padded[plane] = jnp.zeros(padded.shape[1:], jnp.float32)

    def slab_start(chip, which):
        return (chip * CORES + which) * depth

    @pl.loop(0, chips)
    def _(chip):
        own[pl.ds(slab_start(chip, core), depth)] = mine[chip, core]
        own[pl.ds(slab_start(chip, 1 - core), depth)] = theirs[chip, 0]

    @pl.loop(0, chosen.shape[0])
    def _(pair):
        partner = chosen[pair]
        offset = [offsets[pair, axis] for axis in range(3)]
        inside_rows = pl.ds(ROW_PAD, PLANE_ROWS)

        @pl.loop(0, chips)
        def _(chip):
            padded[pl.ds(SHIFT + slab_start(chip, core), depth), inside_rows, :] = mine[
                chip, core + partner
            ]
            padded[pl.ds(SHIFT + slab_start(chip, 1 - core), depth), inside_rows, :] = theirs[
                chip, partner
            ]

        mover[...] = shift_matrix(offset[1] & 1, offset[2])

        @pl.loop(0, chunks)
        def _(chunk):
            at = pl.multiple_of(chunk * CHUNK, CHUNK)
            there = shifted(padded, at, offset, mover[...]).reshape(shape3)
            moved[pl.ds(at, CHUNK)] = there
            start = coulomb_factor * (own[pl.ds(at, CHUNK)] * there)
            residual[pl.ds(at, CHUNK)] = start
            direction = start * (1.0 / centre)
            first[pl.ds(at + 2, CHUNK)] = direction
            total[pl.ds(at, CHUNK)] = direction

        source, target = first, second
        for turn in range(SWEEPS - 1):
            keep_weight, residual_weight = weights[turn]
            last = turn == SWEEPS - 2

            @pl.loop(0, chunks)
            def _(chunk, source=source, target=target, keep=keep_weight, gain=residual_weight, last=last):
                at = pl.multiple_of(chunk * CHUNK, CHUNK)
                window = source[pl.ds(at, CHUNK + 4)]
                applied = operator12(window, stencil[...], CHUNK).reshape(shape3)
                left = residual[pl.ds(at, CHUNK)] - (1.0 / 12.0) * applied
                direction = keep * window[2 : CHUNK + 2] + gain * left
                solved = total[pl.ds(at, CHUNK)] + direction
                if last:
                    own_force[pl.ds(at, CHUNK)] += solved * moved[pl.ds(at, CHUNK)]
                    padded[pl.ds(SHIFT + at, CHUNK), inside_rows, :] = solved * own[pl.ds(at, CHUNK)]
                else:
                    residual[pl.ds(at, CHUNK)] = left
                    target[pl.ds(at + 2, CHUNK)] = direction
                    total[pl.ds(at, CHUNK)] = solved

            source, target = target, source

        back = [-part for part in offset]
        mover[...] = shift_matrix(back[1] & 1, back[2])

        @pl.loop(0, chunks)
        def _(chunk):
            at = pl.multiple_of(chunk * CHUNK, CHUNK)
            there = shifted(padded, at, back, mover[...]).reshape(shape3)
            total[pl.ds(at, CHUNK)] = exact_share * there

        @pl.loop(0, chips)
        def _(chip):
            kept[chip, core + partner] = total[pl.ds(slab_start(chip, core), depth)]
            passed[chip, partner] = total[pl.ds(slab_start(chip, 1 - core), depth)]

    @pl.loop(0, chips)
    def _(chip):
        kept[chip, core] = exact_share * own_force[pl.ds(slab_start(chip, core), depth)]
        passed[chip, 0] = exact_share * own_force[pl.ds(slab_start(chip, 1 - core), depth)]


def pair_forces(chosen, offsets, mine, theirs):
    box = (B, PLANE_ROWS, LANES)
    f32 = jnp.float32
    vmem = pl.BlockSpec(memory_space=pltpu.VMEM)
    smem = pl.BlockSpec(memory_space=pltpu.SMEM)
    return pl.pallas_call(
        pair_kernel,
        out_shape=(
            jax.ShapeDtypeStruct(mine.shape, f32),
            jax.ShapeDtypeStruct(theirs.shape, f32),
        ),
        in_specs=[smem, smem, vmem, vmem],
        out_specs=(vmem, vmem),
        scratch_shapes=[
            pltpu.VMEM((B + 2 * SHIFT, PADDED_ROWS, LANES), f32),
            pltpu.VMEM(box, f32),
            pltpu.VMEM(box, f32),
            pltpu.VMEM((B + 4, PLANE_ROWS, LANES), f32),
            pltpu.VMEM((B + 4, PLANE_ROWS, LANES), f32),
            pltpu.VMEM(box, f32),
            pltpu.VMEM(box, f32),
            pltpu.VMEM(box, f32),
            pltpu.VMEM((2 * LANES, 2 * LANES), jnp.bfloat16),
            pltpu.VMEM((4 * LANES, LANES), jnp.bfloat16),
        ],
        compiler_params=pltpu.CompilerParams(vmem_limit_bytes=56 << 20),
        name="pair_forces",
    )(chosen, offsets, mine, theirs)


def step_kernel(now, before, after, previous, potential, force, advanced):
    depth = now.shape[1]
    window = jnp.concatenate([before[0], now[0], after[0]], axis=0)
    size = math.gcd(depth, CHUNK)
    matrix = stencil_matrix()
    for at in range(0, depth, size):
        applied = operator12(window[at : at + size + 4], matrix, size)
        kinetic = (-0.5 / 12.0) * applied.reshape(size, PLANE_ROWS, LANES)
        part = slice(at, at + size)
        field = now[0, part]
        acceleration = kinetic + force[0, part]
        advanced[0, part] = (
            2.0 * field
            - previous[0, part]
            + verlet_factor * (acceleration - potential[0, part] * field)
        )


def verlet_step(now, before, after, previous, potential, force):
    count = now.shape[0]

    def spec(array):
        return pl.BlockSpec((1,) + array.shape[1:], lambda n: (n, 0, 0, 0))

    operands = (now, before, after, previous, potential, force)
    return pl.pallas_call(
        step_kernel,
        grid=(count,),
        out_shape=jax.ShapeDtypeStruct(now.shape, jnp.float32),
        in_specs=[spec(array) for array in operands],
        out_specs=spec(now),
        name="verlet_step",
    )(*operands)


def from_behind(array, axis, by):
    count = lax.axis_size(axis)
    return lax.ppermute(array, axis, [(i, (i + by) % count) for i in range(count)])


def neighbour_planes(planes):
    count = lax.axis_size("grid")
    depth = planes.shape[1]
    before, after = [], []
    for hop in range(1, -(-2 // depth) + 1):
        size = min(depth, 2 - (hop - 1) * depth)
        forward = [(i, i + hop) for i in range(count - hop)]
        backward = [(i + hop, i) for i in range(count - hop)]
        before.insert(0, lax.ppermute(planes[:, depth - size :], "grid", forward))
        after.append(lax.ppermute(planes[:, :size], "grid", backward))
    return jnp.concatenate(before, axis=1), jnp.concatenate(after, axis=1)


def local(orbitals, previous, potential, partners, offsets):
    slabs = lax.axis_size("grid")
    chips = slabs // CORES
    core = lax.rem(lax.axis_index("grid"), CORES)
    total_orbitals = lax.axis_size(("orb", "grid"))
    group, rows, width = orbitals.shape
    depth = rows // PLANE_ROWS
    planes = orbitals.reshape(group, depth, PLANE_ROWS, width)
    tail = planes.shape[1:]
    steps = AHEAD // CORES
    across = [[chip * CORES + c for chip in range(chips)] for c in range(CORES)]
    swap = [(i, i + 1 - 2 * (i % CORES)) for i in range(slabs)]

    upper = from_behind(planes[:AHEAD], "orb", -1)
    before, after = neighbour_planes(planes)
    blocks = jnp.concatenate([planes, upper], axis=0).reshape((chips + steps, CORES) + tail)
    windows = jnp.concatenate([blocks[s : s + chips] for s in range(steps + 1)], axis=1)
    mine = lax.all_to_all(
        windows, "grid", split_axis=0, concat_axis=0, axis_index_groups=across, tiled=True
    )
    wanted = lax.dynamic_slice_in_dim(mine, 1 - core, 1 + AHEAD, axis=1)
    theirs = lax.ppermute(wanted, "grid", swap)

    first_index = lax.axis_index(("orb", "grid"))
    chosen = jnp.remainder(partners - first_index, total_orbitals).reshape(-1)
    kept, passed = pair_forces(chosen, offsets[0], mine, theirs)

    received = lax.ppermute(passed, "grid", swap)
    summed = kept + lax.dynamic_update_slice_in_dim(
        jnp.zeros_like(kept), received, 1 - core, axis=1
    )
    returned = lax.all_to_all(
        summed, "grid", split_axis=0, concat_axis=0, axis_index_groups=across, tiled=True
    )
    returned = returned.reshape((chips, steps + 1, CORES) + tail)
    folded = sum(
        jnp.pad(returned[:, s], ((s, steps - s),) + ((0, 0),) * (len(tail) + 1))
        for s in range(steps + 1)
    ).reshape(((chips + steps) * CORES,) + tail)
    spilled = from_behind(folded[group:], "orb", 1)
    force = folded[:group] + jnp.pad(spilled, ((0, group - AHEAD),) + ((0, 0),) * len(tail))

    advanced = verlet_step(
        planes, before, after, previous.reshape(planes.shape), potential.reshape(planes.shape), force
    )
    return advanced.reshape(orbitals.shape), force.reshape(orbitals.shape)


def solution(mesh):
    in_specs = (
        P("orb", "grid", None),
        P("orb", "grid", None),
        P("orb", "grid", None),
        P(("orb", "grid"), None),
        P(("orb", "grid"), None, None),
    )
    out_specs = (P("orb", "grid", None), P("orb", "grid", None))
    return jax.shard_map(local, mesh=mesh, in_specs=in_specs, out_specs=out_specs, check_vma=False)
```

time: 639 us -> 265 us (0.41)
  waiting for transfers between devices: 310 us -> 92.9 us
  other arithmetic: 154 us -> 9.69 us
  local copies, waits for them, and re-layouts: 143 us -> 5.6 us
  blocking collectives: 0 us -> 75.5 us
  Pallas kernels: 0 us -> 60.5 us
  starting transfers between devices: 25.9 us -> 15.8 us
    all_to_all x3 -> x1, waiting for transfers between devices: 301 us -> 66.5 us  [local(): lax.all_to_all(windows, 'grid', split_axis=0, concat_axis=0, axis_index_g...]
    all_to_all x0 -> x1, blocking collectives: none -> 75.5 us  [local(): lax.all_to_all(summed, 'grid', split_axis=0, concat_axis=0, axis_index_gr...]
    add x6 -> x3, other arithmetic: 77.9 us -> 5.4 us  [the longest x1 3.86 us: local(): kept + lax.dynamic_update_slice_in_dim(jnp.zeros_like(kept), received, 1...]
    pallas_call x0 -> x2, Pallas kernels: none -> 60.5 us  [the longest x1 53.4 us: pair_forces(): pl.pallas_call(pair_kernel, out_shape=(jax.ShapeDtypeStruct(mine.shape, f...]
    gather x19 -> x0, local copies, waits for them, and re-layouts: 48.4 us -> none
    reduce_sum x1 -> x0, other arithmetic: 43.8 us -> none  [pair_terms(): return (jnp.sum(own_terms, axis=0), partner_terms)]
    pad x2 -> x0, local copies, waits for them, and re-layouts: 21 us -> none  [shift_box(): padded = jnp.pad(one_box, reach_cells)]
    all_to_all x3 -> x1, starting transfers between devices: 21 us -> 5.2 us  [local(): lax.all_to_all(windows, 'grid', split_axis=0, concat_axis=0, axis_index_g...]
  transfers between devices with their start and end apart: 5 -> 7, of which waited for: 4 -> 5; matrix products, arithmetic and copies ran while one was open for 2% -> 1% of each run, Pallas kernels for 0% -> 0%
where the time goes in v1:
time: 265 us; the launch traced here: 261 us
  waiting for transfers between devices  92.9 us (35%)
  blocking collectives  75.5 us (28%)
  Pallas kernels  60.5 us (23%)
  starting transfers between devices  15.8 us (6%)
  other arithmetic  9.69 us (4%)
  local copies, waits for them, and re-layouts  5.6 us (2%)
    all_to_all x1, blocking collectives, local(): lax.all_to_all(summed, 'grid', split_axis=0, concat_axis=0, axis_index_gr...  75.5 us
    all_to_all x1, waiting for transfers between devices, local(): lax.all_to_all(windows, 'grid', split_axis=0, concat_axis=0, axis_index_g...  66.5 us
    pallas_call x1, Pallas kernels, pair_forces(): pl.pallas_call(pair_kernel, out_shape=(jax.ShapeDtypeStruct(mine.shape, f...  53.4 us
    ppermute x2, waiting for transfers between devices, from_behind(): lax.ppermute(array, axis, [(i, (i + by) % count) for i in range(count)])  17.2 us
    pallas_call x1, Pallas kernels, verlet_step(): pl.pallas_call(step_kernel, grid=(count,), out_shape=jax.ShapeDtypeStruct...  7.08 us
  transfers between devices with their start and end apart: 7, of which 5 were waited for; matrix products, arithmetic and copies ran while one was open for 1% of the time, Pallas kernels for 0%

profile of v1, /device:TPU:16, one launch (start us, length us, event | category | flops | bytes accessed | tf_op | source)
XLA Modules:
  0.0 260.7 jit_solution(3361357057741758286)
XLA Ops:
  0.6 0.0 copy-start.1
  0.6 1.2 slice.52
  1.8 2.5 collective-permute-start.2
  4.3 11.2 %collective-permute-done.2 = f32[4,8,32,128]{3,2,1,0:T(8,128)S(1)} collective-permute-done((f32[4,8,32,128]{3,2,1,0:T(8,128)S(1)}, f32[4,8,32,128]{3,2,1,0:T(8,128)S(1)}, u32[]{:S(2)}, u32[]{:S(2)}) %collective-permute-start.2) | collective-permute-done | bytes 524320 | tf_op jit(solution)/shard_map/ppermute | solution.py:277
  15.5 1.6 fusion
  17.1 0.0 copy-done.1
  17.1 2.1 pad_maximum_fusion
  19.3 5.2 %all-to-all-start = ((f32[4,6,8,32,128]{4,3,2,1,0:T(8,128)}), f32[4,6,8,32,128]{4,3,2,1,0:T(8,128)S(1)}, u32[]{:S(2)}, u32[]{:S(2)}) async-start(f32[4,6,8,32,128]{4,3,2,1,0:T(8,128)} %pad_maximum_fusion), calls=%async_computation | async-start | bytes 6291456 | tf_op jit(solution)/shard_map/all_to_all | solution.py:310
  24.5 0.0 copy-start.5
  24.5 0.0 copy-start.6
  24.5 66.5 %all-to-all-done.mine = f32[4,6,8,32,128]{4,3,2,1,0:T(8,128)S(1)} async-done(((f32[4,6,8,32,128]{4,3,2,1,0:T(8,128)}), f32[4,6,8,32,128]{4,3,2,1,0:T(8,128)S(1)}, u32[]{:S(2)}, u32[]{:S(2)}) %all-to-all-start) | async-done | bytes 3145760 | tf_op jit(solution)/shard_map/all_to_all | solution.py:310
  91.0 0.0 copy-start
  91.0 2.1 constant_dynamic-slice_fusion
  93.1 0.4 copy-done
  93.5 0.0 collective-permute-start.3
  93.5 0.0 copy-done.5
  93.5 0.6 copy.15
  94.1 0.0 copy-done.6
  94.1 0.5 fusion.1.chosen
  94.6 4.1 %collective-permute-done.3.theirs = f32[4,5,8,32,128]{4,3,2,1,0:T(8,128)} collective-permute-done((f32[4,5,8,32,128]{4,3,2,1,0:T(8,128)}, f32[4,5,8,32,128]{4,3,2,1,0:T(8,128)}, u32[]{:S(2)}, u32[]{:S(2)}) %collective-permute-start.3) | collective-permute-done | bytes 2621472 | tf_op jit(solution)/shard_map/ppermute | solution.py:314
  98.7 53.4 %pair_forces.1 = (f32[4,6,8,32,128]{4,3,2,1,0:T(8,128)}, f32[4,5,8,32,128]{4,3,2,1,0:T(8,128)}) custom-call(s32[3]{0:T(128)} %fusion.1.chosen, s32[3,3]{1,0:T(4,128)} %bitcast.43, f32[4,6,8,32,128]{4,3,2,1,0:T(8,128)} %copy-done, f32[4,5,8,32,128]{4,3,2,1,0:T(8,128)} %collective-permute-done.3.theirs), custom_call_target="tpu_custom_call" | custom-call | tf_op jit(solution)/shard_map/pair_forces/pallas_call | solution.py:215
  152.2 0.1 collective-permute-start.4
  152.3 5.0 %collective-permute-done.4 = f32[4,5,8,32,128]{4,3,2,1,0:T(8,128)S(1)} collective-permute-done((f32[4,5,8,32,128]{4,3,2,1,0:T(8,128)}, f32[4,5,8,32,128]{4,3,2,1,0:T(8,128)S(1)}, u32[]{:S(2)}, u32[]{:S(2)}) %collective-permute-start.4) | collective-permute-done | bytes 2621472 | tf_op jit(solution)/shard_map/ppermute | solution.py:320
  157.3 3.9 %add_dynamic-update-slice_fusion = f32[4,6,8,32,128]{4,3,2,1,0:T(8,128)} fusion(f32[4,6,8,32,128]{4,3,2,1,0:T(8,128)} %get-tuple-element.4, s32[]{:T(128)S(6)} %select_n.12, f32[4,5,8,32,128]{4,3,2,1,0:T(8,128)S(1)} %collective-permute-done.4), kind=kLoop, calls=%fused_computation.1 | loop fusion | flops 655360 | bytes 7864324 | tf_op jit(solution)/shard_map/add | solution.py:321
  161.1 75.5 %all_to_all.10 = f32[4,6,8,32,128]{4,3,2,1,0:T(8,128)S(1)} all-to-all(f32[4,6,8,32,128]{4,3,2,1,0:T(8,128)} %add_dynamic-update-slice_fusion), channel_id=1, replica_groups={{0,2,4,6},{1,3,5,7},{8,10,12,14},{9,11,13,15},{16,18,20,22},{17,19,21,2..., dimensions={0} | all-to-all | bytes 6291456 | tf_op jit(solution)/shard_map/all_to_all | solution.py:324
  236.6 0.5 slice_bitcast_fusion.2
  237.1 0.0 copy-start.2
  237.1 0.1 pad_add_fusion.1
  237.2 2.4 collective-permute-start.5
  239.6 0.0 copy-done.2
  239.6 1.9 collective-permute-start
  241.6 3.6 %collective-permute-start.1 = (f32[8,2,32,128]{3,2,1,0:T(8,128)S(1)}, f32[8,2,32,128]{3,2,1,0:T(8,128)S(1)}, u32[]{:S(2)}, u32[]{:S(2)}) collective-permute-start(f32[8,2,32,128]{3,2,1,0:T(8,128)S(1)} %get-tuple-element.11), channel_id=1, source_target_pairs={{1,0},{2,1},{3,2},{4,3},{5,4},{6,5},{7,6},{9,8},{10,9},{11,10},{12... | collective-permute-start | bytes 786440 | tf_op jit(solution)/shard_map/ppermute | solution.py:289
  245.2 0.5 pad_add_fusion
  245.7 0.1 slice.72
  245.8 6.0 %collective-permute-done.5 = f32[4,8,32,128]{3,2,1,0:T(8,128)S(1)} collective-permute-done((f32[4,8,32,128]{3,2,1,0:T(8,128)S(1)}, f32[4,8,32,128]{3,2,1,0:T(8,128)S(1)}, u32[]{:S(2)}, u32[]{:S(2)}) %collective-permute-start.5) | collective-permute-done | bytes 524320 | tf_op jit(solution)/shard_map/ppermute | solution.py:277
  251.8 1.1 bitcast_add_fusion.force
  252.8 0.0 collective-permute-done.before
  252.9 0.0 copy-start.3
  252.9 0.0 collective-permute-done.1.after
  252.9 0.0 copy-start.4
  252.9 0.7 copy-done.3
  253.6 0.1 copy-done.4
  253.7 7.1 %verlet_step.1 = f32[8,8,32,128]{3,2,1,0:T(8,128)} custom-call(f32[8,8,32,128]{3,2,1,0:T(8,128)} %bitcast.31, f32[8,2,32,128]{3,2,1,0:T(8,128)} %copy-done.3, f32[8,2,32,128]{3,2,1,0:T(8,128)} %copy-done.4, f32[8,8,32,128]{3,2,1,0:T(8,128)} %bitcast.38, f32[8,8,32,128]{3,2,1,0:T(8,128)} %bitcast.39, f32[8,8,32,128]{3,2,1,0:T(8,128)} %bitcast_add_fusion.force), custom_call_target="tpu_custom_call" | custom-call | tf_op jit(solution)/shard_map/verlet_step/pallas_call | solution.py:265
  (1 shorter events, 0.0 us)
Async XLA Ops:
  0.6 16.5 %copy-start.1 = (f32[8,256,128]{2,1,0:T(8,128)S(1)}, f32[8,256,128]{2,1,0:T(8,128)}, u32[]{:S(2)}) copy-start(f32[8,256,128]{2,1,0:T(8,128)} %param.5) | copy-start | bytes 3145732
  1.8 13.7 %collective-permute-start.2 = (f32[4,8,32,128]{3,2,1,0:T(8,128)S(1)}, f32[4,8,32,128]{3,2,1,0:T(8,128)S(1)}, u32[]{:S(2)}, u32[]{:S(2)}) collective-permute-start(f32[4,8,32,128]{3,2,1,0:T(8,128)S(1)} %bitcast.42), channel_id=1, source_target_pairs={{0,24},{8,0},{16,8},{24,16},{1,25},{9,1},{17,9},{25,17},{2,26},{10... | collective-permute-start | bytes 1572872 | tf_op jit(solution)/shard_map/ppermute | solution.py:277
  19.3 71.7 %all-to-all-start = ((f32[4,6,8,32,128]{4,3,2,1,0:T(8,128)}), f32[4,6,8,32,128]{4,3,2,1,0:T(8,128)S(1)}, u32[]{:S(2)}, u32[]{:S(2)}) async-start(f32[4,6,8,32,128]{4,3,2,1,0:T(8,128)} %pad_maximum_fusion), calls=%async_computation | async-start | bytes 6291456 | tf_op jit(solution)/shard_map/all_to_all | solution.py:310
  24.5 69.0 %copy-start.5 = (s32[1,3,3]{2,0,1:T(1,128)S(1)}, s32[1,3,3]{2,0,1:T(1,128)}, u32[]{:S(2)}) copy-start(s32[1,3,3]{2,0,1:T(1,128)} %param.9) | copy-start | bytes 112
  24.5 69.6 %copy-start.6 = (s32[1,3]{1,0:T(1,128)S(1)}, s32[1,3]{1,0:T(1,128)}, u32[]{:S(2)}) copy-start(s32[1,3]{1,0:T(1,128)} %param.8) | copy-start | bytes 40
  91.0 2.5 copy-start
  93.5 5.3 %collective-permute-start.3 = (f32[4,5,8,32,128]{4,3,2,1,0:T(8,128)}, f32[4,5,8,32,128]{4,3,2,1,0:T(8,128)}, u32[]{:S(2)}, u32[]{:S(2)}) collective-permute-start(f32[4,5,8,32,128]{4,3,2,1,0:T(8,128)} %constant_dynamic-slice_fusion), channel_id=1, source_target_pairs={{0,1},{1,0},{2,3},{3,2},{4,5},{5,4},{6,7},{7,6},{8,9},{9,8},{10,11... | collective-permute-start | bytes 7864328 | tf_op jit(solution)/shard_map/ppermute | solution.py:314
  152.2 5.1 %collective-permute-start.4 = (f32[4,5,8,32,128]{4,3,2,1,0:T(8,128)}, f32[4,5,8,32,128]{4,3,2,1,0:T(8,128)S(1)}, u32[]{:S(2)}, u32[]{:S(2)}) collective-permute-start(f32[4,5,8,32,128]{4,3,2,1,0:T(8,128)} %get-tuple-element.5), channel_id=1, source_target_pairs={{0,1},{1,0},{2,3},{3,2},{4,5},{5,4},{6,7},{7,6},{8,9},{9,8},{10,11... | collective-permute-start | bytes 7864328 | tf_op jit(solution)/shard_map/ppermute | solution.py:320
  237.1 2.5 copy-start.2
  237.2 14.6 %collective-permute-start.5 = (f32[4,8,32,128]{3,2,1,0:T(8,128)S(1)}, f32[4,8,32,128]{3,2,1,0:T(8,128)S(1)}, u32[]{:S(2)}, u32[]{:S(2)}) collective-permute-start(f32[4,8,32,128]{3,2,1,0:T(8,128)S(1)} %bitcast.41), channel_id=1, source_target_pairs={{0,8},{8,16},{16,24},{24,0},{1,9},{9,17},{17,25},{25,1},{2,10},{10... | collective-permute-start | bytes 1572872 | tf_op jit(solution)/shard_map/ppermute | solution.py:277
  239.6 13.2 %collective-permute-start = (f32[8,2,32,128]{3,2,1,0:T(8,128)S(1)}, f32[8,2,32,128]{3,2,1,0:T(8,128)S(1)}, u32[]{:S(2)}, u32[]{:S(2)}) collective-permute-start(f32[8,2,32,128]{3,2,1,0:T(8,128)S(1)} %get-tuple-element.12), channel_id=1, source_target_pairs={{0,1},{1,2},{2,3},{3,4},{4,5},{5,6},{6,7},{8,9},{9,10},{10,11},{11... | collective-permute-start | bytes 786440 | tf_op jit(solution)/shard_map/ppermute | solution.py:288
  241.6 11.3 %collective-permute-start.1 = (f32[8,2,32,128]{3,2,1,0:T(8,128)S(1)}, f32[8,2,32,128]{3,2,1,0:T(8,128)S(1)}, u32[]{:S(2)}, u32[]{:S(2)}) collective-permute-start(f32[8,2,32,128]{3,2,1,0:T(8,128)S(1)} %get-tuple-element.11), channel_id=1, source_target_pairs={{1,0},{2,1},{3,2},{4,3},{5,4},{6,5},{7,6},{9,8},{10,9},{11,10},{12... | collective-permute-start | bytes 786440 | tf_op jit(solution)/shard_map/ppermute | solution.py:289
  252.9 0.7 copy-start.3
  252.9 0.8 copy-start.4

commit v2 on v1

--- a/solution.py
+++ b/solution.py
@@ -15,7 +15,7 @@
 CORES = 2
 LANES = 2 * B
 PLANE_ROWS = B // 2
-CHUNK = 4
+CHUNK = 16
 ROW_PAD = SHIFT // 2
 PADDED_ROWS = PLANE_ROWS + 3 * ROW_PAD
 
@@ -237,38 +237,34 @@
     )(chosen, offsets, mine, theirs)
 
 
-def step_kernel(now, before, after, previous, potential, force, advanced):
+def step_kernel(now, before, after, previous, potential, partial):
     depth = now.shape[1]
     window = jnp.concatenate([before[0], now[0], after[0]], axis=0)
-    size = math.gcd(depth, CHUNK)
-    matrix = stencil_matrix()
-    for at in range(0, depth, size):
-        applied = operator12(window[at : at + size + 4], matrix, size)
-        kinetic = (-0.5 / 12.0) * applied.reshape(size, PLANE_ROWS, LANES)
-        part = slice(at, at + size)
-        field = now[0, part]
-        acceleration = kinetic + force[0, part]
-        advanced[0, part] = (
-            2.0 * field
-            - previous[0, part]
-            + verlet_factor * (acceleration - potential[0, part] * field)
-        )
-
-
-def verlet_step(now, before, after, previous, potential, force):
+    applied = operator12(window, stencil_matrix(), depth)
+    kinetic = (-0.5 / 12.0) * applied.reshape(now.shape[1:])
+    field = now[0]
+    partial[0] = (
+        2.0 * field - previous[0] + verlet_factor * (kinetic - potential[0] * field)
+    )
+
+
+def step_without_force(now, before, after, previous, potential):
     count = now.shape[0]
 
     def spec(array):
         return pl.BlockSpec((1,) + array.shape[1:], lambda n: (n, 0, 0, 0))
 
-    operands = (now, before, after, previous, potential, force)
+    operands = (now, before, after, previous, potential)
     return pl.pallas_call(
         step_kernel,
         grid=(count,),
         out_shape=jax.ShapeDtypeStruct(now.shape, jnp.float32),
         in_specs=[spec(array) for array in operands],
         out_specs=spec(now),
-        name="verlet_step",
+        cost_estimate=pl.CostEstimate(
+            flops=40 * now.size, bytes_accessed=20 * now.size, transcendentals=0
+        ),
+        name="step_without_force",
     )(*operands)
 
 
@@ -306,25 +302,33 @@
     upper = from_behind(planes[:AHEAD], "orb", -1)
     before, after = neighbour_planes(planes)
     blocks = jnp.concatenate([planes, upper], axis=0).reshape((chips + steps, CORES) + tail)
-    windows = jnp.concatenate([blocks[s : s + chips] for s in range(steps + 1)], axis=1)
-    mine = lax.all_to_all(
-        windows, "grid", split_axis=0, concat_axis=0, axis_index_groups=across, tiled=True
-    )
+
+    def exchange(array):
+        return lax.all_to_all(
+            array, "grid", split_axis=0, concat_axis=0, axis_index_groups=across, tiled=True
+        )
+
+    own_group = exchange(planes.reshape((chips, CORES) + tail))
+    ahead = exchange(
+        jnp.concatenate([blocks[s : s + chips] for s in range(1, steps + 1)], axis=1)
+    )
+    mine = jnp.concatenate([own_group, ahead], axis=1)
     wanted = lax.dynamic_slice_in_dim(mine, 1 - core, 1 + AHEAD, axis=1)
     theirs = lax.ppermute(wanted, "grid", swap)
 
     first_index = lax.axis_index(("orb", "grid"))
     chosen = jnp.remainder(partners - first_index, total_orbitals).reshape(-1)
+    partial = step_without_force(
+        planes, before, after, previous.reshape(planes.shape), potential.reshape(planes.shape)
+    )
+    chosen, partial = lax.optimization_barrier((chosen, partial))
     kept, passed = pair_forces(chosen, offsets[0], mine, theirs)
 
     received = lax.ppermute(passed, "grid", swap)
     summed = kept + lax.dynamic_update_slice_in_dim(
         jnp.zeros_like(kept), received, 1 - core, axis=1
     )
-    returned = lax.all_to_all(
-        summed, "grid", split_axis=0, concat_axis=0, axis_index_groups=across, tiled=True
-    )
-    returned = returned.reshape((chips, steps + 1, CORES) + tail)
+    returned = exchange(summed).reshape((chips, steps + 1, CORES) + tail)
     folded = sum(
         jnp.pad(returned[:, s], ((s, steps - s),) + ((0, 0),) * (len(tail) + 1))
         for s in range(steps + 1)
@@ -332,9 +336,7 @@
     spilled = from_behind(folded[group:], "orb", 1)
     force = folded[:group] + jnp.pad(spilled, ((0, group - AHEAD),) + ((0, 0),) * len(tail))
 
-    advanced = verlet_step(
-        planes, before, after, previous.reshape(planes.shape), potential.reshape(planes.shape), force
-    )
+    advanced = partial + verlet_factor * force
     return advanced.reshape(orbitals.shape), force.reshape(orbitals.shape)
 
 

time: 265 us -> 236 us (0.89)
  Pallas kernels: 60.5 us -> 34.5 us
  waiting for transfers between devices: 92.9 us -> 81.4 us
  local copies, waits for them, and re-layouts: 5.6 us -> 11.3 us
  starting transfers between devices: 15.8 us -> 20.8 us
    pallas_call x1, Pallas kernels: 53.4 us -> 27.6 us  [pair_forces(): pl.pallas_call(pair_kernel, out_shape=(jax.ShapeDtypeStruct(mine.shape, f...]
    all_to_all x1 -> x2, waiting for transfers between devices: 66.5 us -> 48.6 us  [exchange(): lax.all_to_all(array, 'grid', split_axis=0, concat_axis=0, axis_index_gro...]
    all_to_all x1 -> x2, starting transfers between devices: 5.2 us -> 12.2 us  [exchange(): lax.all_to_all(array, 'grid', split_axis=0, concat_axis=0, axis_index_gro...]
    ppermute x2, waiting for transfers between devices: 17.2 us -> 23 us  [from_behind(): lax.ppermute(array, axis, [(i, (i + by) % count) for i in range(count)])]
    ppermute x1, waiting for transfers between devices: 4.14 us -> 0.01 us  [local(): theirs = lax.ppermute(wanted, 'grid', swap)]
    ppermute x1, waiting for transfers between devices: 0.01 us -> 3.82 us  [neighbour_planes(): before.insert(0, lax.ppermute(planes[:, depth - size:], 'grid', forward))]
    unnamed x15 -> x16, local copies, waits for them, and re-layouts: 1.76 us -> 4.56 us
  transfers between devices with their start and end apart: 7 -> 8, of which waited for: 5 -> 7; matrix products, arithmetic and copies ran while one was open for 1% -> 3% of each run, Pallas kernels for 0% -> 3%
where the time goes in v2:
time: 236 us; the launch traced here: 232 us
  waiting for transfers between devices  81.4 us (34%)
  blocking collectives  74.6 us (32%)
  Pallas kernels  34.5 us (15%)
  starting transfers between devices  20.8 us (9%)
  local copies, waits for them, and re-layouts  11.3 us (5%)
  other arithmetic  8.17 us (3%)
    all_to_all x1, blocking collectives, exchange(): lax.all_to_all(array, 'grid', split_axis=0, concat_axis=0, axis_index_gro...  74.6 us
    all_to_all x2, waiting for transfers between devices, exchange(): lax.all_to_all(array, 'grid', split_axis=0, concat_axis=0, axis_index_gro...  48.6 us
    pallas_call x1, Pallas kernels, pair_forces(): pl.pallas_call(pair_kernel, out_shape=(jax.ShapeDtypeStruct(mine.shape, f...  27.6 us
    ppermute x2, waiting for transfers between devices, from_behind(): lax.ppermute(array, axis, [(i, (i + by) % count) for i in range(count)])  23 us
    all_to_all x2, starting transfers between devices, exchange(): lax.all_to_all(array, 'grid', split_axis=0, concat_axis=0, axis_index_gro...  12.2 us
    pallas_call x1, Pallas kernels, step_without_force(): pl.pallas_call(step_kernel, grid=(count,), out_shape=jax.ShapeDtypeStruct...  6.86 us
    ppermute x1, waiting for transfers between devices, local(): received = lax.ppermute(passed, 'grid', swap)  5.12 us
  transfers between devices with their start and end apart: 8, of which 7 were waited for; matrix products, arithmetic and copies ran while one was open for 3% of the time, Pallas kernels for 3%

profile of v2, /device:TPU:16, one launch (start us, length us, event | category | flops | bytes accessed | tf_op | source)
XLA Modules:
  0.0 231.5 jit_solution(18051175962574386498)
XLA Ops:
  0.6 0.0 copy-start
  0.6 5.3 %all-to-all-start = ((f32[4,2,8,32,128]{4,3,2,1,0:T(8,128)}), f32[4,2,8,32,128]{4,3,2,1,0:T(8,128)S(1)}, u32[]{:S(2)}, u32[]{:S(2)}) async-start(f32[4,2,8,32,128]{4,3,2,1,0:T(8,128)} %bitcast.29), calls=%async_computation | async-start | bytes 2097152 | tf_op jit(solution)/shard_map/all_to_all | solution.py:307
  6.0 1.1 slice.47
  7.1 2.5 %collective-permute-start.2 = (f32[4,8,32,128]{3,2,1,0:T(8,128)S(1)}, f32[4,8,32,128]{3,2,1,0:T(8,128)S(1)}, u32[]{:S(2)}, u32[]{:S(2)}) collective-permute-start(f32[4,8,32,128]{3,2,1,0:T(8,128)S(1)} %bitcast.41), channel_id=1, source_target_pairs={{0,24},{8,0},{16,8},{24,16},{1,25},{9,1},{17,9},{25,17},{2,26},{10... | collective-permute-start | bytes 1572872 | tf_op jit(solution)/shard_map/ppermute | solution.py:273
  9.6 10.7 %collective-permute-done.2 = f32[4,8,32,128]{3,2,1,0:T(8,128)S(1)} collective-permute-done((f32[4,8,32,128]{3,2,1,0:T(8,128)S(1)}, f32[4,8,32,128]{3,2,1,0:T(8,128)S(1)}, u32[]{:S(2)}, u32[]{:S(2)}) %collective-permute-start.2) | collective-permute-done | bytes 524320 | tf_op jit(solution)/shard_map/ppermute | solution.py:273
  20.3 0.0 copy-done
  20.3 0.3 fusion
  20.5 1.5 pad_maximum_fusion
  22.0 6.4 %all-to-all-done = f32[4,2,8,32,128]{4,3,2,1,0:T(8,128)S(1)} async-done(((f32[4,2,8,32,128]{4,3,2,1,0:T(8,128)}), f32[4,2,8,32,128]{4,3,2,1,0:T(8,128)S(1)}, u32[]{:S(2)}, u32[]{:S(2)}) %all-to-all-start) | async-done | bytes 1048608 | tf_op jit(solution)/shard_map/all_to_all | solution.py:307
  28.4 0.0 copy-start.1
  28.4 1.0 copy-done.1
  29.4 6.9 %all-to-all-start.1 = ((f32[4,4,8,32,128]{4,3,2,1,0:T(8,128)}), f32[4,4,8,32,128]{4,3,2,1,0:T(8,128)S(1)}, u32[]{:S(2)}, u32[]{:S(2)}) async-start(f32[4,4,8,32,128]{4,3,2,1,0:T(8,128)} %pad_maximum_fusion), calls=%async_computation.1 | async-start | bytes 4194304 | tf_op jit(solution)/shard_map/all_to_all | solution.py:307
  36.3 2.3 constant_dynamic-update-slice_fusion.1
  38.5 42.2 %all-to-all-done.1 = f32[4,4,8,32,128]{4,3,2,1,0:T(8,128)S(1)} async-done(((f32[4,4,8,32,128]{4,3,2,1,0:T(8,128)}), f32[4,4,8,32,128]{4,3,2,1,0:T(8,128)S(1)}, u32[]{:S(2)}, u32[]{:S(2)}) %all-to-all-start.1) | async-done | bytes 2097184 | tf_op jit(solution)/shard_map/all_to_all | solution.py:307
  80.7 1.6 constant_dynamic-update-slice_fusion.mine
  82.3 0.0 copy-start.5
  82.3 0.0 copy-start.6
  82.3 3.6 %constant_dynamic-slice_fusion = f32[4,5,8,32,128]{4,3,2,1,0:T(8,128)} fusion(f32[4,6,8,32,128]{4,3,2,1,0:T(8,128)} %constant_dynamic-update-slice_fusion.mine, s32[]{:T(128)S(6)} %select_n.12), kind=kLoop, calls=%fused_computation.19 | loop fusion | bytes 5242884 | tf_op jit(solution)/shard_map/dynamic_slice | solution.py:316
  85.9 0.0 collective-permute-start.3
  86.0 2.6 %collective-permute-start.1 = (f32[8,2,32,128]{3,2,1,0:T(8,128)S(1)}, f32[8,2,32,128]{3,2,1,0:T(8,128)S(1)}, u32[]{:S(2)}, u32[]{:S(2)}) collective-permute-start(f32[8,2,32,128]{3,2,1,0:T(8,128)S(1)} %get-tuple-element.17), channel_id=1, source_target_pairs={{1,0},{2,1},{3,2},{4,3},{5,4},{6,5},{7,6},{9,8},{10,9},{11,10},{12... | collective-permute-start | bytes 786440 | tf_op jit(solution)/shard_map/ppermute | solution.py:285
  88.6 1.9 collective-permute-start
  90.5 0.0 copy-done.5
  90.5 0.6 copy.13
  91.1 0.0 copy-done.6
  91.1 0.5 fusion.1.chosen
  91.6 0.8 collective-permute-done.1.after
  92.5 0.0 copy-start.3
  92.5 3.8 %collective-permute-done.before = f32[8,2,32,128]{3,2,1,0:T(8,128)S(1)} collective-permute-done((f32[8,2,32,128]{3,2,1,0:T(8,128)S(1)}, f32[8,2,32,128]{3,2,1,0:T(8,128)S(1)}, u32[]{:S(2)}, u32[]{:S(2)}) %collective-permute-start) | collective-permute-done | bytes 262176 | tf_op jit(solution)/shard_map/ppermute | solution.py:284
  96.3 0.0 copy-start.4
  96.3 0.0 copy-done.3
  96.3 0.7 copy-done.4
  97.0 6.9 %step_without_force.1 = f32[8,8,32,128]{3,2,1,0:T(8,128)} custom-call(f32[8,8,32,128]{3,2,1,0:T(8,128)} %bitcast.30, f32[8,2,32,128]{3,2,1,0:T(8,128)} %copy-done.4, f32[8,2,32,128]{3,2,1,0:T(8,128)} %copy-done.3, f32[8,8,32,128]{3,2,1,0:T(8,128)} %bitcast.36, f32[8,8,32,128]{3,2,1,0:T(8,128)} %bitcast.37), custom_call_target="tpu_custom_call" | custom-call | flops 10485760 | bytes 5242880 | tf_op jit(solution)/shard_map/step_without_force/pallas_call | solution.py:258
  103.8 0.0 collective-permute-done.3.theirs
  103.8 27.6 %pair_forces.1 = (f32[4,6,8,32,128]{4,3,2,1,0:T(8,128)}, f32[4,5,8,32,128]{4,3,2,1,0:T(8,128)}) custom-call(s32[3]{0:T(128)} %fusion.1.chosen, s32[3,3]{1,0:T(4,128)} %bitcast.42, f32[4,6,8,32,128]{4,3,2,1,0:T(8,128)} %constant_dynamic-update-slice_fusion.mine, f32[4,5,8,32,128]{4,3,2,1,0:T(8,128)} %collective-permute-done.3.theirs), custom_call_target="tpu_custom_call" | custom-call | tf_op jit(solution)/shard_map/pair_forces/pallas_call | solution.py:215
  131.5 0.0 collective-permute-start.4
  131.5 5.1 %collective-permute-done.4 = f32[4,5,8,32,128]{4,3,2,1,0:T(8,128)S(1)} collective-permute-done((f32[4,5,8,32,128]{4,3,2,1,0:T(8,128)}, f32[4,5,8,32,128]{4,3,2,1,0:T(8,128)S(1)}, u32[]{:S(2)}, u32[]{:S(2)}) %collective-permute-start.4) | collective-permute-done | bytes 2621472 | tf_op jit(solution)/shard_map/ppermute | solution.py:327
  136.6 3.9 %add_dynamic-update-slice_fusion = f32[4,6,8,32,128]{4,3,2,1,0:T(8,128)} fusion(f32[4,6,8,32,128]{4,3,2,1,0:T(8,128)} %get-tuple-element.8, s32[]{:T(128)S(6)} %select_n.12, f32[4,5,8,32,128]{4,3,2,1,0:T(8,128)S(1)} %collective-permute-done.4), kind=kLoop, calls=%fused_computation | loop fusion | flops 655360 | bytes 7864324 | tf_op jit(solution)/shard_map/add | solution.py:328
  140.5 74.6 %all_to_all.15 = f32[4,6,8,32,128]{4,3,2,1,0:T(8,128)S(1)} all-to-all(f32[4,6,8,32,128]{4,3,2,1,0:T(8,128)} %add_dynamic-update-slice_fusion), channel_id=1, replica_groups={{0,2,4,6},{1,3,5,7},{8,10,12,14},{9,11,13,15},{16,18,20,22},{17,19,21,2..., dimensions={0} | all-to-all | bytes 6291456 | tf_op jit(solution)/shard_map/all_to_all | solution.py:307
  215.1 0.4 slice_bitcast_fusion.2
  215.5 0.1 pad_add_fusion.1
  215.5 0.0 copy-start.2
  215.5 1.6 collective-permute-start.5
  217.1 0.3 pad_add_fusion
  217.5 0.1 slice.67
  217.6 12.3 %collective-permute-done.5 = f32[4,8,32,128]{3,2,1,0:T(8,128)S(1)} collective-permute-done((f32[4,8,32,128]{3,2,1,0:T(8,128)S(1)}, f32[4,8,32,128]{3,2,1,0:T(8,128)S(1)}, u32[]{:S(2)}, u32[]{:S(2)}) %collective-permute-start.5) | collective-permute-done | bytes 524320 | tf_op jit(solution)/shard_map/ppermute | solution.py:273
  229.9 0.0 copy-done.2
  229.9 1.6 multiply_add_fusion
  (1 shorter events, 0.0 us)
Async XLA Ops:
  0.6 19.6 %copy-start = (f32[8,256,128]{2,1,0:T(8,128)S(1)}, f32[8,256,128]{2,1,0:T(8,128)}, u32[]{:S(2)}) copy-start(f32[8,256,128]{2,1,0:T(8,128)} %param.5) | copy-start | bytes 3145732
  0.6 27.8 %all-to-all-start = ((f32[4,2,8,32,128]{4,3,2,1,0:T(8,128)}), f32[4,2,8,32,128]{4,3,2,1,0:T(8,128)S(1)}, u32[]{:S(2)}, u32[]{:S(2)}) async-start(f32[4,2,8,32,128]{4,3,2,1,0:T(8,128)} %bitcast.29), calls=%async_computation | async-start | bytes 2097152 | tf_op jit(solution)/shard_map/all_to_all | solution.py:307
  7.1 13.2 %collective-permute-start.2 = (f32[4,8,32,128]{3,2,1,0:T(8,128)S(1)}, f32[4,8,32,128]{3,2,1,0:T(8,128)S(1)}, u32[]{:S(2)}, u32[]{:S(2)}) collective-permute-start(f32[4,8,32,128]{3,2,1,0:T(8,128)S(1)} %bitcast.41), channel_id=1, source_target_pairs={{0,24},{8,0},{16,8},{24,16},{1,25},{9,1},{17,9},{25,17},{2,26},{10... | collective-permute-start | bytes 1572872 | tf_op jit(solution)/shard_map/ppermute | solution.py:273
  28.4 1.0 copy-start.1
  29.4 51.3 %all-to-all-start.1 = ((f32[4,4,8,32,128]{4,3,2,1,0:T(8,128)}), f32[4,4,8,32,128]{4,3,2,1,0:T(8,128)S(1)}, u32[]{:S(2)}, u32[]{:S(2)}) async-start(f32[4,4,8,32,128]{4,3,2,1,0:T(8,128)} %pad_maximum_fusion), calls=%async_computation.1 | async-start | bytes 4194304 | tf_op jit(solution)/shard_map/all_to_all | solution.py:307
  82.3 8.2 %copy-start.5 = (s32[1,3,3]{2,0,1:T(1,128)S(1)}, s32[1,3,3]{2,0,1:T(1,128)}, u32[]{:S(2)}) copy-start(s32[1,3,3]{2,0,1:T(1,128)} %param.9) | copy-start | bytes 112
  82.3 8.8 %copy-start.6 = (s32[1,3]{1,0:T(1,128)S(1)}, s32[1,3]{1,0:T(1,128)}, u32[]{:S(2)}) copy-start(s32[1,3]{1,0:T(1,128)} %param.8) | copy-start | bytes 40
  85.9 17.9 %collective-permute-start.3 = (f32[4,5,8,32,128]{4,3,2,1,0:T(8,128)}, f32[4,5,8,32,128]{4,3,2,1,0:T(8,128)}, u32[]{:S(2)}, u32[]{:S(2)}) collective-permute-start(f32[4,5,8,32,128]{4,3,2,1,0:T(8,128)} %constant_dynamic-slice_fusion), channel_id=1, source_target_pairs={{0,1},{1,0},{2,3},{3,2},{4,5},{5,4},{6,7},{7,6},{8,9},{9,8},{10,11... | collective-permute-start | bytes 7864328 | tf_op jit(solution)/shard_map/ppermute | solution.py:317
  86.0 6.5 %collective-permute-start.1 = (f32[8,2,32,128]{3,2,1,0:T(8,128)S(1)}, f32[8,2,32,128]{3,2,1,0:T(8,128)S(1)}, u32[]{:S(2)}, u32[]{:S(2)}) collective-permute-start(f32[8,2,32,128]{3,2,1,0:T(8,128)S(1)} %get-tuple-element.17), channel_id=1, source_target_pairs={{1,0},{2,1},{3,2},{4,3},{5,4},{6,5},{7,6},{9,8},{10,9},{11,10},{12... | collective-permute-start | bytes 786440 | tf_op jit(solution)/shard_map/ppermute | solution.py:285
  88.6 7.7 %collective-permute-start = (f32[8,2,32,128]{3,2,1,0:T(8,128)S(1)}, f32[8,2,32,128]{3,2,1,0:T(8,128)S(1)}, u32[]{:S(2)}, u32[]{:S(2)}) collective-permute-start(f32[8,2,32,128]{3,2,1,0:T(8,128)S(1)} %get-tuple-element.18), channel_id=1, source_target_pairs={{0,1},{1,2},{2,3},{3,4},{4,5},{5,6},{6,7},{8,9},{9,10},{10,11},{11... | collective-permute-start | bytes 786440 | tf_op jit(solution)/shard_map/ppermute | solution.py:284
  92.5 3.8 %copy-start.3 = (f32[8,2,32,128]{3,2,1,0:T(8,128)}, f32[8,2,32,128]{3,2,1,0:T(8,128)S(1)}, u32[]{:S(2)}) copy-start(f32[8,2,32,128]{3,2,1,0:T(8,128)S(1)} %collective-permute-done.1.after) | copy-start | bytes 786436
  96.3 0.7 copy-start.4
  131.5 5.1 %collective-permute-start.4 = (f32[4,5,8,32,128]{4,3,2,1,0:T(8,128)}, f32[4,5,8,32,128]{4,3,2,1,0:T(8,128)S(1)}, u32[]{:S(2)}, u32[]{:S(2)}) collective-permute-start(f32[4,5,8,32,128]{4,3,2,1,0:T(8,128)} %get-tuple-element.9), channel_id=1, source_target_pairs={{0,1},{1,0},{2,3},{3,2},{4,5},{5,4},{6,7},{7,6},{8,9},{9,8},{10,11... | collective-permute-start | bytes 7864328 | tf_op jit(solution)/shard_map/ppermute | solution.py:327
  215.5 14.4 %copy-start.2 = (f32[8,8,32,128]{3,2,1,0:T(8,128)S(1)}, f32[8,8,32,128]{3,2,1,0:T(8,128)}, u32[]{:S(2)}) copy-start(f32[8,8,32,128]{3,2,1,0:T(8,128)} %step_without_force.1) | copy-start | bytes 3145732
  215.5 14.4 %collective-permute-start.5 = (f32[4,8,32,128]{3,2,1,0:T(8,128)S(1)}, f32[4,8,32,128]{3,2,1,0:T(8,128)S(1)}, u32[]{:S(2)}, u32[]{:S(2)}) collective-permute-start(f32[4,8,32,128]{3,2,1,0:T(8,128)S(1)} %bitcast.40), channel_id=1, source_target_pairs={{0,8},{8,16},{16,24},{24,0},{1,9},{9,17},{17,25},{25,1},{2,10},{10... | collective-permute-start | bytes 1572872 | tf_op jit(solution)/shard_map/ppermute | solution.py:273

commit v3 on v2

--- a/solution.py
+++ b/solution.py
@@ -12,6 +12,8 @@
 SWEEPS = 4
 AHEAD = 4
 SHIFT = 16
+RELAY_ITEMS = 32
+MESH = pl.DeviceIdType.MESH
 CORES = 2
 LANES = 2 * B
 PLANE_ROWS = B // 2
@@ -111,6 +113,9 @@
 ):
     chips, _, depth = mine.shape[:3]
     core = lax.rem(lax.axis_index("grid"), CORES)
+    base = core
+    if mine.shape[1] > theirs.shape[1]:
+        base = lax.axis_index("grid")
     chunks = B // CHUNK
     centre, weights = sweep_weights()
     shape3 = (CHUNK, PLANE_ROWS, LANES)
@@ -133,8 +138,8 @@
 
     @pl.loop(0, chips)
     def _(chip):
-        own[pl.ds(slab_start(chip, core), depth)] = mine[chip, core]
-        own[pl.ds(slab_start(chip, 1 - core), depth)] = theirs[chip, 0]
+        own[pl.ds(slab_start(chip, core), depth)] = mine[chip, base]
+        own[pl.ds(slab_start(chip, 1 - core), depth)] = theirs[chip, core]
 
     @pl.loop(0, chosen.shape[0])
     def _(pair):
@@ -145,10 +150,10 @@
         @pl.loop(0, chips)
         def _(chip):
             padded[pl.ds(SHIFT + slab_start(chip, core), depth), inside_rows, :] = mine[
-                chip, core + partner
+                chip, base + partner
             ]
             padded[pl.ds(SHIFT + slab_start(chip, 1 - core), depth), inside_rows, :] = theirs[
-                chip, partner
+                chip, core + partner
             ]
 
         mover[...] = shift_matrix(offset[1] & 1, offset[2])
@@ -199,12 +204,12 @@
         @pl.loop(0, chips)
         def _(chip):
             kept[chip, core + partner] = total[pl.ds(slab_start(chip, core), depth)]
-            passed[chip, partner] = total[pl.ds(slab_start(chip, 1 - core), depth)]
+            passed[chip, core + partner] = total[pl.ds(slab_start(chip, 1 - core), depth)]
 
     @pl.loop(0, chips)
     def _(chip):
         kept[chip, core] = exact_share * own_force[pl.ds(slab_start(chip, core), depth)]
-        passed[chip, 0] = exact_share * own_force[pl.ds(slab_start(chip, 1 - core), depth)]
+        passed[chip, core] = exact_share * own_force[pl.ds(slab_start(chip, 1 - core), depth)]
 
 
 def pair_forces(chosen, offsets, mine, theirs):
@@ -215,7 +220,7 @@
     return pl.pallas_call(
         pair_kernel,
         out_shape=(
-            jax.ShapeDtypeStruct(mine.shape, f32),
+            jax.ShapeDtypeStruct(theirs.shape, f32),
             jax.ShapeDtypeStruct(theirs.shape, f32),
         ),
         in_specs=[smem, smem, vmem, vmem],
@@ -232,7 +237,7 @@
             pltpu.VMEM((2 * LANES, 2 * LANES), jnp.bfloat16),
             pltpu.VMEM((4 * LANES, LANES), jnp.bfloat16),
         ],
-        compiler_params=pltpu.CompilerParams(vmem_limit_bytes=56 << 20),
+        compiler_params=pltpu.CompilerParams(vmem_limit_bytes=60 << 20),
         name="pair_forces",
     )(chosen, offsets, mine, theirs)
 
@@ -268,6 +273,335 @@
     )(*operands)
 
 
+def position():
+    orb, grid = lax.axis_index("orb"), lax.axis_index("grid")
+    return orb, grid, grid // CORES, lax.rem(grid, CORES)
+
+
+def greet(devices):
+    barrier = pltpu.get_barrier_semaphore()
+    for there, device in devices:
+
+        @pl.when(there)
+        def _(device=device):
+            pl.semaphore_signal(barrier, inc=1, device_id=device, device_id_type=MESH)
+
+    pl.semaphore_wait(barrier, sum(there.astype(jnp.int32) for there, _ in devices))
+
+
+def gather_kernel(
+    planes, held, other, local_sem, up_send, right_send, left_send, recv, swap_send, swap_recv
+):
+    chips, items = held.shape[:2]
+    steps = items - chips
+    orb, grid, chip, core = position()
+    orbs = lax.axis_size("orb")
+    sibling = (orb, grid + 1 - 2 * core)
+    right, left = (orb, grid + CORES), (orb, grid - CORES)
+    up, down = (lax.rem(orb + 1, orbs), grid), (lax.rem(orb + orbs - 1, orbs), grid)
+    has_right, has_left, always = chip < chips - 1, chip > 0, chip >= 0
+    greet([(always, sibling), (has_right, right), (has_left, left), (always, up), (always, down)])
+
+    def remote(source, target, sent, landed, device):
+        return pltpu.make_async_remote_copy(
+            src_ref=source, dst_ref=target, send_sem=sent, recv_sem=landed,
+            device_id=device, device_id_type=MESH,
+        )
+
+    def upward(j):
+        k = chips + j
+        return remote(planes.at[j], held.at[chip, k], up_send.at[j], recv.at[chip, k], down)
+
+    def rightward(s, k, source):
+        return remote(source, held.at[s, k], right_send.at[s, k], recv.at[s, k], right)
+
+    def leftward(s, k, source):
+        return remote(source, held.at[s, k], left_send.at[s, k], recv.at[s, k], left)
+
+    def across(s, j, source):
+        return remote(source, other.at[s, j], swap_send.at[s, j], swap_recv.at[s, j], sibling)
+
+    def goes_right(k):
+        return has_right & (k >= chip + 1)
+
+    def goes_left(k):
+        return has_left & (k <= chip - 1 + steps)
+
+    def wanted(k):
+        return (k >= chip) & (k <= chip + steps)
+
+    for j in range(steps):
+        upward(j).start()
+    keep = pltpu.make_async_copy(planes, held.at[chip, pl.ds(0, chips)], local_sem)
+    keep.start()
+
+    for first, last, own in ((0, chips, True), (chips, items, False)):
+
+        @pl.loop(first, last)
+        def _(k, own=own):
+            source = planes.at[k] if own else held.at[chip, k]
+            if not own:
+                upward(k - chips).wait_recv()
+
+            @pl.when(goes_right(k))
+            def _():
+                rightward(chip, k, source).start()
+
+            @pl.when(goes_left(k))
+            def _():
+                leftward(chip, k, source).start()
+
+            @pl.when(wanted(k))
+            def _():
+                across(chip, k - chip, source).start()
+
+        for hop in range(1, chips):
+
+            @pl.loop(first, last)
+            def _(k, hop=hop):
+                s = chip - hop
+
+                @pl.when((chip >= hop) & (k >= chip))
+                def _():
+                    item = held.at[s, k]
+                    rightward(s, k, item).wait_recv()
+
+                    @pl.when(goes_right(k))
+                    def _():
+                        rightward(s, k, item).start()
+
+                    @pl.when(wanted(k))
+                    def _():
+                        across(s, k - chip, item).start()
+
+                t = chip + hop
+
+                @pl.when((t < chips) & (k <= chip + steps))
+                def _():
+                    item = held.at[t, k]
+                    leftward(t, k, item).wait_recv()
+
+                    @pl.when(goes_left(k))
+                    def _():
+                        leftward(t, k, item).start()
+
+                    @pl.when(wanted(k))
+                    def _():
+                        across(t, k - chip, item).start()
+
+    keep.wait()
+    for j in range(steps):
+        upward(j).wait_send()
+
+    @pl.loop(0, chips)
+    def _(s):
+        @pl.loop(0, items)
+        def _(k):
+            item = planes.at[0]
+
+            @pl.when(goes_right(k) & (s <= chip))
+            def _():
+                rightward(s, k, item).wait_send()
+
+            @pl.when(goes_left(k) & (s >= chip))
+            def _():
+                leftward(s, k, item).wait_send()
+
+        @pl.loop(0, steps + 1)
+        def _(j):
+            across(s, j, planes.at[0]).wait()
+
+
+def gather_boxes(planes, steps):
+    chips = planes.shape[0]
+    items = chips + steps
+    tail = planes.shape[1:]
+    anywhere = pl.BlockSpec(memory_space=pl.ANY)
+    dma = pltpu.SemaphoreType.DMA
+    return pl.pallas_call(
+        gather_kernel,
+        out_shape=(
+            jax.ShapeDtypeStruct((chips, items) + tail, planes.dtype),
+            jax.ShapeDtypeStruct((chips, steps + 1) + tail, planes.dtype),
+        ),
+        in_specs=[pl.BlockSpec(memory_space=pltpu.VMEM)],
+        out_specs=(anywhere, anywhere),
+        scratch_shapes=[
+            dma, dma((steps,)), dma((chips, items)), dma((chips, items)), dma((chips, items)),
+            dma((chips, steps + 1)), dma((chips, steps + 1)),
+        ],
+        compiler_params=pltpu.CompilerParams(
+            collective_id=0, has_side_effects=True, vmem_limit_bytes=8 << 20
+        ),
+        name="gather_boxes",
+    )(planes)
+
+
+def return_kernel(
+    kept, passed, folded, sibling_in, left_in, right_in,
+    swap_send, swap_recv, left_send, left_recv, right_send, right_recv,
+):
+    chips, items = left_in.shape[:2]
+    steps = items - chips
+    orb, grid, chip, core = position()
+    sibling = (orb, grid + 1 - 2 * core)
+    right, left = (orb, grid + CORES), (orb, grid - CORES)
+    has_right, has_left, always = chip < chips - 1, chip > 0, chip >= 0
+    greet([(always, sibling), (has_right, right), (has_left, left)])
+
+    def remote(source, target, sent, landed, device):
+        return pltpu.make_async_remote_copy(
+            src_ref=source, dst_ref=target, send_sem=sent, recv_sem=landed,
+            device_id=device, device_id_type=MESH,
+        )
+
+    def across(s, j):
+        return remote(
+            passed.at[s, j], sibling_in.at[s, j], swap_send.at[s, j], swap_recv.at[s, j], sibling
+        )
+
+    def leftward(s, k):
+        return remote(
+            left_in.at[s, k], left_in.at[s, k], left_send.at[s, k], left_recv.at[s, k], left
+        )
+
+    def rightward(s, k):
+        return remote(
+            right_in.at[s, k], right_in.at[s, k], right_send.at[s, k], right_recv.at[s, k], right
+        )
+
+    def from_right(k):
+        return has_right & (k >= chip + 1)
+
+    def from_left(k):
+        return has_left & (k <= chip - 1 + steps)
+
+    def contributes(k):
+        return (k >= chip) & (k <= chip + steps)
+
+    def share(s, k):
+        return kept[s, k - chip] + sibling_in[s, k - chip]
+
+    for turn in range(chips):
+        for s, leaves in ((turn, chip > turn), (chips - 1 - turn, chip < chips - 1 - turn)):
+
+            @pl.loop(0, steps + 1)
+            def _(j, s=s, leaves=leaves):
+                @pl.when(leaves)
+                def _():
+                    across(s, j).start()
+
+    @pl.loop(0, steps + 1)
+    def _(j):
+        across(chip, j).start()
+
+    for turn in range(chips - 1):
+
+        @pl.loop(0, items)
+        def _(k, s=turn):
+            @pl.when((s < chip) & (k >= chip))
+            def _():
+                @pl.when(contributes(k))
+                def _():
+                    across(s, k - chip).wait_recv()
+
+                @pl.when(from_right(k))
+                def _():
+                    leftward(s, k).wait_recv()
+
+                    @pl.when(contributes(k))
+                    def _():
+                        left_in[s, k] += share(s, k)
+
+                @pl.when(jnp.logical_not(from_right(k)))
+                def _():
+                    left_in[s, k] = share(s, k)
+
+                leftward(s, k).start()
+
+        @pl.loop(0, items)
+        def _(k, s=chips - 1 - turn):
+            @pl.when((s > chip) & (k <= chip + steps))
+            def _():
+                @pl.when(contributes(k))
+                def _():
+                    across(s, k - chip).wait_recv()
+
+                @pl.when(from_left(k))
+                def _():
+                    rightward(s, k).wait_recv()
+
+                    @pl.when(contributes(k))
+                    def _():
+                        right_in[s, k] += share(s, k)
+
+                @pl.when(jnp.logical_not(from_left(k)))
+                def _():
+                    right_in[s, k] = share(s, k)
+
+                rightward(s, k).start()
+
+    @pl.loop(0, items)
+    def _(k):
+        folded[k] = jnp.zeros(folded.shape[1:], folded.dtype)
+
+        @pl.when(contributes(k))
+        def _():
+            across(chip, k - chip).wait_recv()
+            folded[k] = share(chip, k)
+
+        @pl.when(from_right(k))
+        def _():
+            leftward(chip, k).wait_recv()
+            folded[k] += left_in[chip, k]
+
+        @pl.when(from_left(k))
+        def _():
+            rightward(chip, k).wait_recv()
+            folded[k] += right_in[chip, k]
+
+    @pl.loop(0, chips)
+    def _(s):
+        @pl.loop(0, steps + 1)
+        def _(j):
+            across(s, j).wait_send()
+
+        @pl.loop(0, items)
+        def _(k):
+            @pl.when((s < chip) & (k >= chip))
+            def _():
+                leftward(s, k).wait_send()
+
+            @pl.when((s > chip) & (k <= chip + steps))
+            def _():
+                rightward(s, k).wait_send()
+
+
+def return_forces(kept, passed):
+    chips, span = kept.shape[:2]
+    items = chips + span - 1
+    tail = kept.shape[2:]
+    vmem = pl.BlockSpec(memory_space=pltpu.VMEM)
+    dma = pltpu.SemaphoreType.DMA
+    line = (chips, items)
+    return pl.pallas_call(
+        return_kernel,
+        out_shape=jax.ShapeDtypeStruct((items,) + tail, kept.dtype),
+        in_specs=[vmem, vmem],
+        out_specs=vmem,
+        scratch_shapes=[
+            pltpu.VMEM(kept.shape, kept.dtype),
+            pltpu.VMEM(line + tail, kept.dtype),
+            pltpu.VMEM(line + tail, kept.dtype),
+            dma((chips, span)), dma((chips, span)), dma(line), dma(line), dma(line), dma(line),
+        ],
+        compiler_params=pltpu.CompilerParams(
+            collective_id=1, has_side_effects=True, vmem_limit_bytes=40 << 20
+        ),
+        name="return_forces",
+    )(kept, passed)
+
+
 def from_behind(array, axis, by):
     count = lax.axis_size(axis)
     return lax.ppermute(array, axis, [(i, (i + by) % count) for i in range(count)])
@@ -289,7 +623,6 @@
 def local(orbitals, previous, potential, partners, offsets):
     slabs = lax.axis_size("grid")
     chips = slabs // CORES
-    core = lax.rem(lax.axis_index("grid"), CORES)
     total_orbitals = lax.axis_size(("orb", "grid"))
     group, rows, width = orbitals.shape
     depth = rows // PLANE_ROWS
@@ -299,22 +632,29 @@
     across = [[chip * CORES + c for chip in range(chips)] for c in range(CORES)]
     swap = [(i, i + 1 - 2 * (i % CORES)) for i in range(slabs)]
 
-    upper = from_behind(planes[:AHEAD], "orb", -1)
     before, after = neighbour_planes(planes)
-    blocks = jnp.concatenate([planes, upper], axis=0).reshape((chips + steps, CORES) + tail)
+    by_chip = (chips, CORES) + tail
+    boxes = (CORES * (steps + 1),) + tail
+    relayed = chips * (chips + steps) <= RELAY_ITEMS
 
     def exchange(array):
         return lax.all_to_all(
             array, "grid", split_axis=0, concat_axis=0, axis_index_groups=across, tiled=True
         )
 
-    own_group = exchange(planes.reshape((chips, CORES) + tail))
-    ahead = exchange(
-        jnp.concatenate([blocks[s : s + chips] for s in range(1, steps + 1)], axis=1)
-    )
-    mine = jnp.concatenate([own_group, ahead], axis=1)
-    wanted = lax.dynamic_slice_in_dim(mine, 1 - core, 1 + AHEAD, axis=1)
-    theirs = lax.ppermute(wanted, "grid", swap)
+    if relayed:
+        mine, theirs = gather_boxes(planes.reshape(by_chip), steps)
+        mine = mine.reshape((chips, CORES * (chips + steps)) + tail)
+        theirs = theirs.reshape((chips,) + boxes)
+    else:
+        upper = from_behind(planes[:AHEAD], "orb", -1)
+        blocks = jnp.concatenate([planes, upper], axis=0).reshape((chips + steps, CORES) + tail)
+        own_group = exchange(planes.reshape(by_chip))
+        ahead = exchange(
+            jnp.concatenate([blocks[s : s + chips] for s in range(1, steps + 1)], axis=1)
+        )
+        mine = jnp.concatenate([own_group, ahead], axis=1)
+        theirs = lax.ppermute(mine, "grid", swap)
 
     first_index = lax.axis_index(("orb", "grid"))
     chosen = jnp.remainder(partners - first_index, total_orbitals).reshape(-1)
@@ -324,15 +664,17 @@
     chosen, partial = lax.optimization_barrier((chosen, partial))
     kept, passed = pair_forces(chosen, offsets[0], mine, theirs)
 
-    received = lax.ppermute(passed, "grid", swap)
-    summed = kept + lax.dynamic_update_slice_in_dim(
-        jnp.zeros_like(kept), received, 1 - core, axis=1
-    )
-    returned = exchange(summed).reshape((chips, steps + 1, CORES) + tail)
-    folded = sum(
-        jnp.pad(returned[:, s], ((s, steps - s),) + ((0, 0),) * (len(tail) + 1))
-        for s in range(steps + 1)
-    ).reshape(((chips + steps) * CORES,) + tail)
+    if relayed:
+        pairs = (chips, steps + 1, CORES) + tail
+        folded = return_forces(kept.reshape(pairs), passed.reshape(pairs))
+    else:
+        summed = kept + lax.ppermute(passed, "grid", swap)
+        returned = exchange(summed).reshape((chips, steps + 1, CORES) + tail)
+        folded = sum(
+            jnp.pad(returned[:, s], ((s, steps - s),) + ((0, 0),) * (len(tail) + 1))
+            for s in range(steps + 1)
+        )
+    folded = folded.reshape(((chips + steps) * CORES,) + tail)
     spilled = from_behind(folded[group:], "orb", 1)
     force = folded[:group] + jnp.pad(spilled, ((0, group - AHEAD),) + ((0, 0),) * len(tail))
 

time: 236 us -> 229 us (0.970); the launches traced: 232 us -> 228 us
  Pallas kernels: 34.5 us -> 195 us
  blocking collectives: 74.6 us -> 0 us
  waiting for transfers between devices: 81.4 us -> 12 us
  starting transfers between devices: 20.8 us -> 5.22 us
  other arithmetic: 8.17 us -> 2.81 us
    pallas_call x1 -> x3, Pallas kernels: 27.6 us -> 188 us  [the longest x1 81.2 us: gather_boxes(): pl.pallas_call(gather_kernel, out_shape=(jax.ShapeDtypeStruct((chips, ite...]
    all_to_all x1 -> x0, blocking collectives: 74.6 us -> none  [exchange(): lax.all_to_all(array, 'grid', split_axis=0, concat_axis=0, axis_index_gro...]
    all_to_all x2 -> x0, waiting for transfers between devices: 48.6 us -> none  [exchange(): lax.all_to_all(array, 'grid', split_axis=0, concat_axis=0, axis_index_gro...]
    all_to_all x2 -> x0, starting transfers between devices: 12.2 us -> none  [exchange(): lax.all_to_all(array, 'grid', split_axis=0, concat_axis=0, axis_index_gro...]
    ppermute x2 -> x1, waiting for transfers between devices: 23 us -> 12 us  [from_behind(): lax.ppermute(array, axis, [(i, (i + by) % count) for i in range(count)])]
    unnamed x16 -> x17, local copies, waits for them, and re-layouts: 4.56 us -> 11.3 us
    ppermute x2 -> x0, waiting for transfers between devices: 5.12 us -> none  [the longest x1 5.12 us: local(): received = lax.ppermute(passed, 'grid', swap)]
    add x2 -> x0, other arithmetic: 4.22 us -> none  [the longest x1 3.87 us: local(): kept + lax.dynamic_update_slice_in_dim(jnp.zeros_like(kept), received, 1...]
  transfers between devices with their start and end apart: 8 -> 3, of which waited for: 7 -> 1; matrix products, arithmetic and copies ran while one was open for 3% -> 1% of each run, Pallas kernels for 3% -> 36%
where the time goes in v3:
time: 229 us; the launch traced here: 228 us
  Pallas kernels  195 us (85%)
  local copies, waits for them, and re-layouts  12.6 us (6%)
  waiting for transfers between devices  12 us (5%)
  starting transfers between devices  5.22 us (2%)
  other arithmetic  2.81 us (1%)
    pallas_call x1, Pallas kernels, gather_boxes(): pl.pallas_call(gather_kernel, out_shape=(jax.ShapeDtypeStruct((chips, ite...  81.2 us
    pallas_call x1, Pallas kernels, return_forces(): pl.pallas_call(return_kernel, out_shape=jax.ShapeDtypeStruct((items,) + t...  77.5 us
    pallas_call x1, Pallas kernels, pair_forces(): pl.pallas_call(pair_kernel, out_shape=(jax.ShapeDtypeStruct(theirs.shape,...  29 us
    ppermute x1, waiting for transfers between devices, from_behind(): lax.ppermute(array, axis, [(i, (i + by) % count) for i in range(count)])  12 us
    unnamed x17, local copies, waits for them, and re-layouts  11.3 us
    pallas_call x1, Pallas kernels, step_without_force(): pl.pallas_call(step_kernel, grid=(count,), out_shape=jax.ShapeDtypeStruct...  6.86 us
  transfers between devices with their start and end apart: 3, of which 1 were waited for; matrix products, arithmetic and copies ran while one was open for 1% of the time, Pallas kernels for 36%

profile of v3, /device:TPU:16, one launch (start us, length us, event | category | flops | bytes accessed | tf_op | source)
XLA Modules:
  0.0 227.9 jit_solution(14688702871479565225)
XLA Ops:
  0.6 1.1 fusion.2
  1.7 1.9 collective-permute-start.1
  3.6 2.4 %collective-permute-start = (f32[8,2,32,128]{3,2,1,0:T(8,128)S(1)}, f32[8,2,32,128]{3,2,1,0:T(8,128)S(1)}, u32[]{:S(2)}, u32[]{:S(2)}) collective-permute-start(f32[8,2,32,128]{3,2,1,0:T(8,128)S(1)} %get-tuple-element.17), channel_id=1, source_target_pairs={{0,1},{1,2},{2,3},{3,4},{4,5},{5,6},{6,7},{8,9},{9,10},{10,11},{11... | collective-permute-start | bytes 786440 | tf_op jit(solution)/shard_map/ppermute | solution.py:618
  6.1 1.2 copy.9
  7.3 0.0 copy-start
  7.3 1.2 copy-done
  8.5 81.2 %gather_boxes.1 = (f32[4,6,2,8,32,128]{5,4,3,2,1,0:T(8,128)S(1)}, f32[4,3,2,8,32,128]{5,4,3,2,1,0:T(8,128)S(1)}) custom-call(f32[4,2,8,32,128]{4,3,2,1,0:T(8,128)S(1)} %bitcast.21), custom_call_target="tpu_custom_call" | custom-call | tf_op jit(solution)/shard_map/gather_boxes/pallas_call | solution.py:421
  89.7 0.0 copy-start.1
  89.7 2.6 %copy-done.1 = f32[4,6,2,8,32,128]{5,4,3,2,1,0:T(8,128)} copy-done((f32[4,6,2,8,32,128]{5,4,3,2,1,0:T(8,128)}, f32[4,6,2,8,32,128]{5,4,3,2,1,0:T(8,128)S(1)}, u32[]{:S(2)}) %copy-start.1) | copy-done | bytes 6291480
  92.4 0.0 copy-start.2
  92.4 1.7 copy-done.2
  94.1 1.2 fusion.chosen
  95.3 0.0 collective-permute-done.1.after
  95.3 0.0 copy-start.6
  95.3 0.0 collective-permute-done.before
  95.3 0.0 copy-start.7
  95.3 0.7 copy-done.6
  96.0 0.1 copy-done.7
  96.1 6.9 %step_without_force.1 = f32[8,8,32,128]{3,2,1,0:T(8,128)} custom-call(f32[8,8,32,128]{3,2,1,0:T(8,128)} %bitcast.20, f32[8,2,32,128]{3,2,1,0:T(8,128)} %copy-done.7, f32[8,2,32,128]{3,2,1,0:T(8,128)} %copy-done.6, f32[8,8,32,128]{3,2,1,0:T(8,128)} %bitcast.26, f32[8,8,32,128]{3,2,1,0:T(8,128)} %bitcast.27), custom_call_target="tpu_custom_call" | custom-call | flops 10485760 | bytes 5242880 | tf_op jit(solution)/shard_map/step_without_force/pallas_call | solution.py:263
  102.9 29.0 %pair_forces.1 = (f32[4,6,8,32,128]{4,3,2,1,0:T(8,128)}, f32[4,6,8,32,128]{4,3,2,1,0:T(8,128)}) custom-call(s32[3]{0:T(128)} %fusion.chosen, s32[3,3]{1,0:T(4,128)} %bitcast.31, f32[4,12,8,32,128]{4,3,2,1,0:T(8,128)} %bitcast.22, f32[4,6,8,32,128]{4,3,2,1,0:T(8,128)} %bitcast.23), custom_call_target="tpu_custom_call" | custom-call | tf_op jit(solution)/shard_map/pair_forces/pallas_call | solution.py:220
  132.0 0.0 copy-start.3
  132.0 1.9 copy-done.3
  133.8 0.0 copy-start.4
  133.8 1.9 copy-done.4
  135.7 77.5 %return_forces.1 = f32[6,2,8,32,128]{4,3,2,1,0:T(8,128)S(1)} custom-call(f32[4,3,2,8,32,128]{5,4,3,2,1,0:T(8,128)S(1)} %bitcast.24, f32[4,3,2,8,32,128]{5,4,3,2,1,0:T(8,128)S(1)} %bitcast.25), custom_call_target="tpu_custom_call" | custom-call | tf_op jit(solution)/shard_map/return_forces/pallas_call | solution.py:587
  213.2 0.0 copy-start.5
  213.3 0.9 collective-permute-start.2
  214.2 0.1 slice.20
  214.3 12.0 %collective-permute-done.2 = f32[4,8,32,128]{3,2,1,0:T(8,128)S(1)} collective-permute-done((f32[4,8,32,128]{3,2,1,0:T(8,128)S(1)}, f32[4,8,32,128]{3,2,1,0:T(8,128)S(1)}, u32[]{:S(2)}, u32[]{:S(2)}) %collective-permute-start.2) | collective-permute-done | bytes 524320 | tf_op jit(solution)/shard_map/ppermute | solution.py:607
  226.3 0.0 copy-done.5
  226.3 1.6 multiply_add_fusion
  (1 shorter events, 0.0 us)
Async XLA Ops:
  1.7 93.6 %collective-permute-start.1 = (f32[8,2,32,128]{3,2,1,0:T(8,128)S(1)}, f32[8,2,32,128]{3,2,1,0:T(8,128)S(1)}, u32[]{:S(2)}, u32[]{:S(2)}) collective-permute-start(f32[8,2,32,128]{3,2,1,0:T(8,128)S(1)} %get-tuple-element.16), channel_id=1, source_target_pairs={{1,0},{2,1},{3,2},{4,3},{5,4},{6,5},{7,6},{9,8},{10,9},{11,10},{12... | collective-permute-start | bytes 786440 | tf_op jit(solution)/shard_map/ppermute | solution.py:619
  3.6 91.6 %collective-permute-start = (f32[8,2,32,128]{3,2,1,0:T(8,128)S(1)}, f32[8,2,32,128]{3,2,1,0:T(8,128)S(1)}, u32[]{:S(2)}, u32[]{:S(2)}) collective-permute-start(f32[8,2,32,128]{3,2,1,0:T(8,128)S(1)} %get-tuple-element.17), channel_id=1, source_target_pairs={{0,1},{1,2},{2,3},{3,4},{4,5},{5,6},{6,7},{8,9},{9,10},{10,11},{11... | collective-permute-start | bytes 786440 | tf_op jit(solution)/shard_map/ppermute | solution.py:618
  7.3 1.2 copy-start
  89.7 2.6 %copy-start.1 = (f32[4,6,2,8,32,128]{5,4,3,2,1,0:T(8,128)}, f32[4,6,2,8,32,128]{5,4,3,2,1,0:T(8,128)S(1)}, u32[]{:S(2)}) copy-start(f32[4,6,2,8,32,128]{5,4,3,2,1,0:T(8,128)S(1)} %get-tuple-element.10) | copy-start | bytes 18874372
  92.4 1.7 copy-start.2
  95.3 0.7 copy-start.6
  95.3 0.8 copy-start.7
  132.0 1.9 copy-start.3
  133.8 1.9 copy-start.4
  213.2 13.1 %copy-start.5 = (f32[8,8,32,128]{3,2,1,0:T(8,128)S(1)}, f32[8,8,32,128]{3,2,1,0:T(8,128)}, u32[]{:S(2)}) copy-start(f32[8,8,32,128]{3,2,1,0:T(8,128)} %step_without_force.1) | copy-start | bytes 3145732
  213.3 13.0 %collective-permute-start.2 = (f32[4,8,32,128]{3,2,1,0:T(8,128)S(1)}, f32[4,8,32,128]{3,2,1,0:T(8,128)S(1)}, u32[]{:S(2)}, u32[]{:S(2)}) collective-permute-start(f32[4,8,32,128]{3,2,1,0:T(8,128)S(1)} %bitcast.30), channel_id=1, source_target_pairs={{0,8},{8,16},{16,24},{24,0},{1,9},{9,17},{17,25},{25,1},{2,10},{10... | collective-permute-start | bytes 1572872 | tf_op jit(solution)/shard_map/ppermute | solution.py:607

commit v4 on v3

--- a/solution.py
+++ b/solution.py
@@ -273,6 +273,42 @@
     )(*operands)
 
 
+LINK_TIME = 5.6
+HOP_TIME = 2.0
+UPPER_TIME = 12.0
+
+
+def arrival_orders(chips, steps, gathering):
+    items = chips + steps
+    pending, orders, free = [], [[] for _ in range(chips)], {}
+    for chip in range(chips):
+        for flow in (1, -1):
+            for s in range(chips):
+                for k in range(items):
+                    if gathering:
+                        starts = s == chip
+                        last = min(k, chips - 1) if flow > 0 else max(0, k - steps)
+                        hops = (last - chip) * flow
+                        ready = 0.0 if k < chips else UPPER_TIME
+                    else:
+                        hops = (s - chip) * flow
+                        alone = k == chip + steps if flow > 0 else k == chip
+                        edge = chip == 0 if flow > 0 else chip == chips - 1
+                        starts = chip <= k <= chip + steps and (alone or edge)
+                        ready = 1.0
+                    if starts and hops > 0:
+                        pending.append((ready, -hops, chip, flow, s, k, hops))
+    while pending:
+        pending.sort()
+        ready, _, chip, flow, s, k, hops = pending.pop(0)
+        orders[chip].append((ready, flow, s, k))
+        if hops > 0:
+            sent = max(ready, free.get((chip, flow), 0.0)) + LINK_TIME
+            free[chip, flow] = sent
+            pending.append((sent + HOP_TIME, 1 - hops, chip + flow, flow, s, k, hops - 1))
+    return orders
+
+
 def position():
     orb, grid = lax.axis_index("orb"), lax.axis_index("grid")
     return orb, grid, grid // CORES, lax.rem(grid, CORES)
@@ -335,59 +371,32 @@
     keep = pltpu.make_async_copy(planes, held.at[chip, pl.ds(0, chips)], local_sem)
     keep.start()
 
-    for first, last, own in ((0, chips, True), (chips, items, False)):
-
-        @pl.loop(first, last)
-        def _(k, own=own):
-            source = planes.at[k] if own else held.at[chip, k]
-            if not own:
-                upward(k - chips).wait_recv()
-
-            @pl.when(goes_right(k))
-            def _():
-                rightward(chip, k, source).start()
-
-            @pl.when(goes_left(k))
-            def _():
-                leftward(chip, k, source).start()
-
-            @pl.when(wanted(k))
-            def _():
-                across(chip, k - chip, source).start()
-
-        for hop in range(1, chips):
-
-            @pl.loop(first, last)
-            def _(k, hop=hop):
-                s = chip - hop
-
-                @pl.when((chip >= hop) & (k >= chip))
-                def _():
-                    item = held.at[s, k]
-                    rightward(s, k, item).wait_recv()
-
-                    @pl.when(goes_right(k))
-                    def _():
-                        rightward(s, k, item).start()
-
-                    @pl.when(wanted(k))
-                    def _():
-                        across(s, k - chip, item).start()
-
-                t = chip + hop
-
-                @pl.when((t < chips) & (k <= chip + steps))
-                def _():
-                    item = held.at[t, k]
-                    leftward(t, k, item).wait_recv()
-
-                    @pl.when(goes_left(k))
-                    def _():
-                        leftward(t, k, item).start()
-
-                    @pl.when(wanted(k))
-                    def _():
-                        across(t, k - chip, item).start()
+    for here, order in enumerate(arrival_orders(chips, steps, True)):
+
+        @pl.when(chip == here)
+        def _(here=here, order=order):
+            arrived, swapped = set(), set()
+            for _, flow, slab, k in order:
+                own = slab == here
+                item = planes.at[k] if own and k < chips else held.at[slab, k]
+                send = rightward if flow > 0 else leftward
+                if own and k >= chips and k not in arrived:
+                    upward(k - chips).wait_recv()
+                    arrived.add(k)
+                if not own:
+                    send(slab, k, item).wait_recv()
+                onward = here + 1 <= min(k, chips - 1) if flow > 0 else here - 1 >= max(0, k - steps)
+                if onward:
+                    send(slab, k, item).start()
+                if here <= k <= here + steps and (slab, k) not in swapped:
+                    across(slab, k - here, item).start()
+                    swapped.add((slab, k))
+            for k in range(chips, items):
+                if k not in arrived:
+                    upward(k - chips).wait_recv()
+            for k in range(here, here + steps + 1):
+                if (here, k) not in swapped:
+                    across(here, k - here, planes.at[k] if k < chips else held.at[here, k]).start()
 
     keep.wait()
     for j in range(steps):
@@ -495,51 +504,25 @@
     def _(j):
         across(chip, j).start()
 
-    for turn in range(chips - 1):
-
-        @pl.loop(0, items)
-        def _(k, s=turn):
-            @pl.when((s < chip) & (k >= chip))
-            def _():
-                @pl.when(contributes(k))
-                def _():
-                    across(s, k - chip).wait_recv()
-
-                @pl.when(from_right(k))
-                def _():
-                    leftward(s, k).wait_recv()
-
-                    @pl.when(contributes(k))
-                    def _():
-                        left_in[s, k] += share(s, k)
-
-                @pl.when(jnp.logical_not(from_right(k)))
-                def _():
-                    left_in[s, k] = share(s, k)
-
-                leftward(s, k).start()
-
-        @pl.loop(0, items)
-        def _(k, s=chips - 1 - turn):
-            @pl.when((s > chip) & (k <= chip + steps))
-            def _():
-                @pl.when(contributes(k))
-                def _():
-                    across(s, k - chip).wait_recv()
-
-                @pl.when(from_left(k))
-                def _():
-                    rightward(s, k).wait_recv()
-
-                    @pl.when(contributes(k))
-                    def _():
-                        right_in[s, k] += share(s, k)
-
-                @pl.when(jnp.logical_not(from_left(k)))
-                def _():
-                    right_in[s, k] = share(s, k)
-
-                rightward(s, k).start()
+    for here, order in enumerate(arrival_orders(chips, steps, False)):
+
+        @pl.when(chip == here)
+        def _(here=here, order=order):
+            swapped = set()
+            for _, flow, slab, k in order:
+                if slab == here:
+                    continue
+                buffer, send = (right_in, rightward) if flow > 0 else (left_in, leftward)
+                alone = (here == 0 or k == here + steps) if flow > 0 else (here == chips - 1 or k == here)
+                if not alone:
+                    send(slab, k).wait_recv()
+                if here <= k <= here + steps:
+                    if (slab, k) not in swapped:
+                        across(slab, k - here).wait_recv()
+                        swapped.add((slab, k))
+                    added = kept[slab, k - here] + sibling_in[slab, k - here]
+                    buffer[slab, k] = added if alone else buffer[slab, k] + added
+                send(slab, k).start()
 
     @pl.loop(0, items)
     def _(k):

time: 229 us -> 187 us (0.82)
  Pallas kernels: 195 us -> 151 us
    pallas_call x1, Pallas kernels: 81.2 us -> 57 us  [gather_boxes(): pl.pallas_call(gather_kernel, out_shape=(jax.ShapeDtypeStruct((chips, ite...]
    pallas_call x1, Pallas kernels: 77.5 us -> 58.5 us  [return_forces(): pl.pallas_call(return_kernel, out_shape=jax.ShapeDtypeStruct((items,) + t...]
  transfers between devices with their start and end apart: 3 -> 3, of which waited for: 1 -> 1; matrix products, arithmetic and copies ran while one was open for 1% -> 1% of each run, Pallas kernels for 36% -> 31%
where the time goes in v4:
time: 187 us; the launch traced here: 186 us
  Pallas kernels  151 us (81%)
  waiting for transfers between devices  13.7 us (7%)
  local copies, waits for them, and re-layouts  12.6 us (7%)
  starting transfers between devices  5.1 us (3%)
  other arithmetic  2.81 us (2%)
    pallas_call x1, Pallas kernels, return_forces(): pl.pallas_call(return_kernel, out_shape=jax.ShapeDtypeStruct((items,) + t...  58.5 us
    pallas_call x1, Pallas kernels, gather_boxes(): pl.pallas_call(gather_kernel, out_shape=(jax.ShapeDtypeStruct((chips, ite...  57 us
    pallas_call x1, Pallas kernels, pair_forces(): pl.pallas_call(pair_kernel, out_shape=(jax.ShapeDtypeStruct(theirs.shape,...  29 us
    ppermute x1, waiting for transfers between devices, from_behind(): lax.ppermute(array, axis, [(i, (i + by) % count) for i in range(count)])  13.7 us
    unnamed x17, local copies, waits for them, and re-layouts  11.4 us
    pallas_call x1, Pallas kernels, step_without_force(): pl.pallas_call(step_kernel, grid=(count,), out_shape=jax.ShapeDtypeStruct...  6.86 us
  transfers between devices with their start and end apart: 3, of which 1 were waited for; matrix products, arithmetic and copies ran while one was open for 1% of the time, Pallas kernels for 31%

profile of v4, /device:TPU:16, one launch (start us, length us, event | category | flops | bytes accessed | tf_op | source)
XLA Modules:
  0.0 186.2 jit_solution(6014257799537647143)
XLA Ops:
  0.6 1.1 fusion.2
  1.7 1.9 %collective-permute-start.1 = (f32[8,2,32,128]{3,2,1,0:T(8,128)S(1)}, f32[8,2,32,128]{3,2,1,0:T(8,128)S(1)}, u32[]{:S(2)}, u32[]{:S(2)}) collective-permute-start(f32[8,2,32,128]{3,2,1,0:T(8,128)S(1)} %get-tuple-element.16), channel_id=1, source_target_pairs={{1,0},{2,1},{3,2},{4,3},{5,4},{6,5},{7,6},{9,8},{10,9},{11,10},{12... | collective-permute-start | bytes 786440 | tf_op jit(solution)/shard_map/ppermute | solution.py:602
  3.6 2.4 %collective-permute-start = (f32[8,2,32,128]{3,2,1,0:T(8,128)S(1)}, f32[8,2,32,128]{3,2,1,0:T(8,128)S(1)}, u32[]{:S(2)}, u32[]{:S(2)}) collective-permute-start(f32[8,2,32,128]{3,2,1,0:T(8,128)S(1)} %get-tuple-element.17), channel_id=1, source_target_pairs={{0,1},{1,2},{2,3},{3,4},{4,5},{5,6},{6,7},{8,9},{9,10},{10,11},{11... | collective-permute-start | bytes 786440 | tf_op jit(solution)/shard_map/ppermute | solution.py:601
  6.1 1.2 copy.9
  7.3 0.0 copy-start
  7.3 1.2 copy-done
  8.5 57.0 %gather_boxes.1 = (f32[4,6,2,8,32,128]{5,4,3,2,1,0:T(8,128)S(1)}, f32[4,3,2,8,32,128]{5,4,3,2,1,0:T(8,128)S(1)}) custom-call(f32[4,2,8,32,128]{4,3,2,1,0:T(8,128)S(1)} %bitcast.21), custom_call_target="tpu_custom_call" | custom-call | tf_op jit(solution)/shard_map/gather_boxes/pallas_call | solution.py:430
  65.5 0.0 copy-start.1
  65.5 2.6 %copy-done.1 = f32[4,6,2,8,32,128]{5,4,3,2,1,0:T(8,128)} copy-done((f32[4,6,2,8,32,128]{5,4,3,2,1,0:T(8,128)}, f32[4,6,2,8,32,128]{5,4,3,2,1,0:T(8,128)S(1)}, u32[]{:S(2)}) %copy-start.1) | copy-done | bytes 6291480
  68.1 0.0 copy-start.2
  68.1 1.7 copy-done.2
  69.8 1.2 fusion.chosen
  71.0 0.0 collective-permute-done.1.after
  71.0 0.0 copy-start.6
  71.0 0.0 collective-permute-done.before
  71.0 0.0 copy-start.7
  71.0 0.7 copy-done.6
  71.7 0.1 copy-done.7
  71.8 6.9 %step_without_force.1 = f32[8,8,32,128]{3,2,1,0:T(8,128)} custom-call(f32[8,8,32,128]{3,2,1,0:T(8,128)} %bitcast.20, f32[8,2,32,128]{3,2,1,0:T(8,128)} %copy-done.7, f32[8,2,32,128]{3,2,1,0:T(8,128)} %copy-done.6, f32[8,8,32,128]{3,2,1,0:T(8,128)} %bitcast.26, f32[8,8,32,128]{3,2,1,0:T(8,128)} %bitcast.27), custom_call_target="tpu_custom_call" | custom-call | flops 10485760 | bytes 5242880 | tf_op jit(solution)/shard_map/step_without_force/pallas_call | solution.py:263
  78.7 29.0 %pair_forces.1 = (f32[4,6,8,32,128]{4,3,2,1,0:T(8,128)}, f32[4,6,8,32,128]{4,3,2,1,0:T(8,128)}) custom-call(s32[3]{0:T(128)} %fusion.chosen, s32[3,3]{1,0:T(4,128)} %bitcast.31, f32[4,12,8,32,128]{4,3,2,1,0:T(8,128)} %bitcast.22, f32[4,6,8,32,128]{4,3,2,1,0:T(8,128)} %bitcast.23), custom_call_target="tpu_custom_call" | custom-call | tf_op jit(solution)/shard_map/pair_forces/pallas_call | solution.py:220
  107.6 0.0 copy-start.3
  107.6 1.9 %copy-done.3 = f32[4,6,8,32,128]{4,3,2,1,0:T(8,128)S(1)} copy-done((f32[4,6,8,32,128]{4,3,2,1,0:T(8,128)S(1)}, f32[4,6,8,32,128]{4,3,2,1,0:T(8,128)}, u32[]{:S(2)}) %copy-start.3) | copy-done | bytes 3145752
  109.5 0.0 copy-start.4
  109.5 1.9 %copy-done.4 = f32[4,6,8,32,128]{4,3,2,1,0:T(8,128)S(1)} copy-done((f32[4,6,8,32,128]{4,3,2,1,0:T(8,128)S(1)}, f32[4,6,8,32,128]{4,3,2,1,0:T(8,128)}, u32[]{:S(2)}) %copy-start.4) | copy-done | bytes 3145752
  111.4 58.5 %return_forces.1 = f32[6,2,8,32,128]{4,3,2,1,0:T(8,128)S(1)} custom-call(f32[4,3,2,8,32,128]{5,4,3,2,1,0:T(8,128)S(1)} %bitcast.24, f32[4,3,2,8,32,128]{5,4,3,2,1,0:T(8,128)S(1)} %bitcast.25), custom_call_target="tpu_custom_call" | custom-call | tf_op jit(solution)/shard_map/return_forces/pallas_call | solution.py:570
  169.9 0.0 copy-start.5
  170.0 0.8 collective-permute-start.2
  170.8 0.1 slice.20
  170.9 13.7 %collective-permute-done.2 = f32[4,8,32,128]{3,2,1,0:T(8,128)S(1)} collective-permute-done((f32[4,8,32,128]{3,2,1,0:T(8,128)S(1)}, f32[4,8,32,128]{3,2,1,0:T(8,128)S(1)}, u32[]{:S(2)}, u32[]{:S(2)}) %collective-permute-start.2) | collective-permute-done | bytes 524320 | tf_op jit(solution)/shard_map/ppermute | solution.py:590
  184.6 0.0 copy-done.5
  184.6 1.6 multiply_add_fusion
  (1 shorter events, 0.0 us)
Async XLA Ops:
  1.7 69.3 %collective-permute-start.1 = (f32[8,2,32,128]{3,2,1,0:T(8,128)S(1)}, f32[8,2,32,128]{3,2,1,0:T(8,128)S(1)}, u32[]{:S(2)}, u32[]{:S(2)}) collective-permute-start(f32[8,2,32,128]{3,2,1,0:T(8,128)S(1)} %get-tuple-element.16), channel_id=1, source_target_pairs={{1,0},{2,1},{3,2},{4,3},{5,4},{6,5},{7,6},{9,8},{10,9},{11,10},{12... | collective-permute-start | bytes 786440 | tf_op jit(solution)/shard_map/ppermute | solution.py:602
  3.6 67.4 %collective-permute-start = (f32[8,2,32,128]{3,2,1,0:T(8,128)S(1)}, f32[8,2,32,128]{3,2,1,0:T(8,128)S(1)}, u32[]{:S(2)}, u32[]{:S(2)}) collective-permute-start(f32[8,2,32,128]{3,2,1,0:T(8,128)S(1)} %get-tuple-element.17), channel_id=1, source_target_pairs={{0,1},{1,2},{2,3},{3,4},{4,5},{5,6},{6,7},{8,9},{9,10},{10,11},{11... | collective-permute-start | bytes 786440 | tf_op jit(solution)/shard_map/ppermute | solution.py:601
  7.3 1.2 copy-start
  65.5 2.6 %copy-start.1 = (f32[4,6,2,8,32,128]{5,4,3,2,1,0:T(8,128)}, f32[4,6,2,8,32,128]{5,4,3,2,1,0:T(8,128)S(1)}, u32[]{:S(2)}) copy-start(f32[4,6,2,8,32,128]{5,4,3,2,1,0:T(8,128)S(1)} %get-tuple-element.10) | copy-start | bytes 18874372
  68.1 1.7 copy-start.2
  71.0 0.7 copy-start.6
  71.0 0.8 copy-start.7
  107.6 1.9 %copy-start.3 = (f32[4,6,8,32,128]{4,3,2,1,0:T(8,128)S(1)}, f32[4,6,8,32,128]{4,3,2,1,0:T(8,128)}, u32[]{:S(2)}) copy-start(f32[4,6,8,32,128]{4,3,2,1,0:T(8,128)} %get-tuple-element.12) | copy-start | bytes 9437188
  109.5 1.9 %copy-start.4 = (f32[4,6,8,32,128]{4,3,2,1,0:T(8,128)S(1)}, f32[4,6,8,32,128]{4,3,2,1,0:T(8,128)}, u32[]{:S(2)}) copy-start(f32[4,6,8,32,128]{4,3,2,1,0:T(8,128)} %get-tuple-element.13) | copy-start | bytes 9437188
  169.9 14.6 %copy-start.5 = (f32[8,8,32,128]{3,2,1,0:T(8,128)S(1)}, f32[8,8,32,128]{3,2,1,0:T(8,128)}, u32[]{:S(2)}) copy-start(f32[8,8,32,128]{3,2,1,0:T(8,128)} %step_without_force.1) | copy-start | bytes 3145732
  170.0 14.6 %collective-permute-start.2 = (f32[4,8,32,128]{3,2,1,0:T(8,128)S(1)}, f32[4,8,32,128]{3,2,1,0:T(8,128)S(1)}, u32[]{:S(2)}, u32[]{:S(2)}) collective-permute-start(f32[4,8,32,128]{3,2,1,0:T(8,128)S(1)} %bitcast.30), channel_id=1, source_target_pairs={{0,8},{8,16},{16,24},{24,0},{1,9},{9,17},{17,25},{25,1},{2,10},{10... | collective-permute-start | bytes 1572872 | tf_op jit(solution)/shard_map/ppermute | solution.py:590

commit v5 on v4

--- a/solution.py
+++ b/solution.py
@@ -17,7 +17,7 @@
 CORES = 2
 LANES = 2 * B
 PLANE_ROWS = B // 2
-CHUNK = 16
+CHUNK = 32
 ROW_PAD = SHIFT // 2
 PADDED_ROWS = PLANE_ROWS + 3 * ROW_PAD
 
@@ -237,15 +237,19 @@
             pltpu.VMEM((2 * LANES, 2 * LANES), jnp.bfloat16),
             pltpu.VMEM((4 * LANES, LANES), jnp.bfloat16),
         ],
-        compiler_params=pltpu.CompilerParams(vmem_limit_bytes=60 << 20),
+        compiler_params=pltpu.CompilerParams(vmem_limit_bytes=36 << 20),
         name="pair_forces",
     )(chosen, offsets, mine, theirs)
 
 
-def step_kernel(now, before, after, previous, potential, partial):
+def step_kernel(now, before, after, previous, potential, partial, stencil):
+    @pl.when(pl.program_id(0) == 0)
+    def _():
+        stencil[...] = stencil_matrix()
+
     depth = now.shape[1]
     window = jnp.concatenate([before[0], now[0], after[0]], axis=0)
-    applied = operator12(window, stencil_matrix(), depth)
+    applied = operator12(window, stencil[...], depth)
     kinetic = (-0.5 / 12.0) * applied.reshape(now.shape[1:])
     field = now[0]
     partial[0] = (
@@ -266,9 +270,11 @@
         out_shape=jax.ShapeDtypeStruct(now.shape, jnp.float32),
         in_specs=[spec(array) for array in operands],
         out_specs=spec(now),
+        scratch_shapes=[pltpu.VMEM((2 * LANES, 2 * LANES), jnp.bfloat16)],
         cost_estimate=pl.CostEstimate(
             flops=40 * now.size, bytes_accessed=20 * now.size, transcendentals=0
         ),
+        compiler_params=pltpu.CompilerParams(vmem_limit_bytes=12 << 20),
         name="step_without_force",
     )(*operands)
 
@@ -579,7 +585,7 @@
             dma((chips, span)), dma((chips, span)), dma(line), dma(line), dma(line), dma(line),
         ],
         compiler_params=pltpu.CompilerParams(
-            collective_id=1, has_side_effects=True, vmem_limit_bytes=40 << 20
+            collective_id=1, has_side_effects=True, vmem_limit_bytes=26 << 20
         ),
         name="return_forces",
     )(kept, passed)

time: 187 us -> 174 us (0.930)
  Pallas kernels: 151 us -> 139 us
    pallas_call x1, Pallas kernels: 29 us -> 18.7 us  [pair_forces(): pl.pallas_call(pair_kernel, out_shape=(jax.ShapeDtypeStruct(theirs.shape,...]
    pallas_call x1, Pallas kernels: 6.86 us -> 4.36 us  [step_without_force(): pl.pallas_call(step_kernel, grid=(count,), out_shape=jax.ShapeDtypeStruct...]
    unnamed x17 -> x13, local copies, waits for them, and re-layouts: 11.4 us -> 11 us
  transfers between devices with their start and end apart: 3 -> 3, of which waited for: 1 -> 1; matrix products, arithmetic and copies ran while one was open for 1% -> 1% of each run, Pallas kernels for 31% -> 33%
where the time goes in v5:
time: 174 us; the launch traced here: 173 us
  Pallas kernels  139 us (80%)
  waiting for transfers between devices  13.6 us (8%)
  local copies, waits for them, and re-layouts  13 us (7%)
  starting transfers between devices  5.12 us (3%)
  other arithmetic  2.29 us (1%)
    pallas_call x1, Pallas kernels, return_forces(): pl.pallas_call(return_kernel, out_shape=jax.ShapeDtypeStruct((items,) + t...  58.6 us
    pallas_call x1, Pallas kernels, gather_boxes(): pl.pallas_call(gather_kernel, out_shape=(jax.ShapeDtypeStruct((chips, ite...  57 us
    pallas_call x1, Pallas kernels, pair_forces(): pl.pallas_call(pair_kernel, out_shape=(jax.ShapeDtypeStruct(theirs.shape,...  18.7 us
    ppermute x1, waiting for transfers between devices, from_behind(): lax.ppermute(array, axis, [(i, (i + by) % count) for i in range(count)])  13.6 us
    unnamed x13, local copies, waits for them, and re-layouts  11 us
    pallas_call x1, Pallas kernels, step_without_force(): pl.pallas_call(step_kernel, grid=(count,), out_shape=jax.ShapeDtypeStruct...  4.36 us
  transfers between devices with their start and end apart: 3, of which 1 were waited for; matrix products, arithmetic and copies ran while one was open for 1% of the time, Pallas kernels for 33%

profile of v5, /device:TPU:16, one launch (start us, length us, event | category | flops | bytes accessed | tf_op | source)
XLA Modules:
  0.0 173.4 jit_solution(15405066325650842958)
XLA Ops:
  0.6 1.9 %fusion.2 = (f32[8,2,32,128]{3,2,1,0:T(8,128)}, f32[8,2,32,128]{3,2,1,0:T(8,128)}) fusion(f32[8,8,32,128]{3,2,1,0:T(8,128)} %bitcast.19), kind=kLoop, calls=%fused_computation.8 | loop fusion | bytes 1048576 | tf_op jit(solution)/shard_map/slice | solution.py:608
  2.5 1.9 %collective-permute-start.1 = (f32[8,2,32,128]{3,2,1,0:T(8,128)}, f32[8,2,32,128]{3,2,1,0:T(8,128)S(1)}, u32[]{:S(2)}, u32[]{:S(2)}) collective-permute-start(f32[8,2,32,128]{3,2,1,0:T(8,128)} %get-tuple-element.16), channel_id=1, source_target_pairs={{1,0},{2,1},{3,2},{4,3},{5,4},{6,5},{7,6},{9,8},{10,9},{11,10},{12... | collective-permute-start | bytes 786440 | tf_op jit(solution)/shard_map/ppermute | solution.py:608
  4.4 2.4 %collective-permute-start = (f32[8,2,32,128]{3,2,1,0:T(8,128)}, f32[8,2,32,128]{3,2,1,0:T(8,128)}, u32[]{:S(2)}, u32[]{:S(2)}) collective-permute-start(f32[8,2,32,128]{3,2,1,0:T(8,128)} %get-tuple-element.17), channel_id=1, source_target_pairs={{0,1},{1,2},{2,3},{3,4},{4,5},{5,6},{6,7},{8,9},{9,10},{10,11},{11... | collective-permute-start | bytes 786440 | tf_op jit(solution)/shard_map/ppermute | solution.py:607
  6.8 0.7 copy.9
  7.5 0.0 copy-start
  7.5 1.2 copy-done
  8.7 57.0 %gather_boxes.1 = (f32[4,6,2,8,32,128]{5,4,3,2,1,0:T(8,128)S(1)}, f32[4,3,2,8,32,128]{5,4,3,2,1,0:T(8,128)S(1)}) custom-call(f32[4,2,8,32,128]{4,3,2,1,0:T(8,128)S(1)} %bitcast.20), custom_call_target="tpu_custom_call" | custom-call | tf_op jit(solution)/shard_map/gather_boxes/pallas_call | solution.py:436
  65.7 0.0 copy-start.2
  65.7 2.6 %copy-done.2 = f32[4,6,2,8,32,128]{5,4,3,2,1,0:T(8,128)} copy-done((f32[4,6,2,8,32,128]{5,4,3,2,1,0:T(8,128)}, f32[4,6,2,8,32,128]{5,4,3,2,1,0:T(8,128)S(1)}, u32[]{:S(2)}) %copy-start.2) | copy-done | bytes 6291480
  68.4 0.7 fusion.chosen
  69.0 0.0 collective-permute-done.1.after
  69.0 0.0 collective-permute-done.before
  69.0 0.0 copy-start.1
  69.1 1.2 copy-done.1
  70.3 0.0 copy-start.4
  70.3 1.2 copy-done.4
  71.5 0.0 copy-start.5
  71.5 1.2 copy-done.5
  72.7 4.4 %step_without_force.1 = f32[8,8,32,128]{3,2,1,0:T(8,128)S(1)} custom-call(f32[8,8,32,128]{3,2,1,0:T(8,128)S(1)} %bitcast.21, f32[8,2,32,128]{3,2,1,0:T(8,128)} %collective-permute-done.before, f32[8,2,32,128]{3,2,1,0:T(8,128)S(1)} %collective-permute-done.1.after, f32[8,8,32,128]{3,2,1,0:T(8,128)S(1)} %bitcast.26, f32[8,8,32,128]{3,2,1,0:T(8,128)S(1)} %bitcast.27), custom_call_target="tpu_custom_call" | custom-call | flops 10485760 | bytes 5242880 | tf_op jit(solution)/shard_map/step_without_force/pallas_call | solution.py:267
  77.1 0.0 copy-start.3
  77.1 2.8 %copy-done.3 = f32[4,6,2,8,32,128]{5,4,3,2,1,0:T(8,128)S(1)} copy-done((f32[4,6,2,8,32,128]{5,4,3,2,1,0:T(8,128)S(1)}, f32[4,6,2,8,32,128]{5,4,3,2,1,0:T(8,128)}, u32[]{:S(2)}) %copy-start.3) | copy-done | bytes 6291480
  79.9 18.7 %pair_forces.1 = (f32[4,6,8,32,128]{4,3,2,1,0:T(8,128)S(1)}, f32[4,6,8,32,128]{4,3,2,1,0:T(8,128)S(1)}) custom-call(s32[3]{0:T(128)S(1)} %fusion.chosen, s32[3,3]{1,0:T(4,128)S(1)} %bitcast.28, f32[4,12,8,32,128]{4,3,2,1,0:T(8,128)S(1)} %bitcast.22, f32[4,6,8,32,128]{4,3,2,1,0:T(8,128)S(1)} %bitcast.23), custom_call_target="tpu_custom_call" | custom-call | tf_op jit(solution)/shard_map/pair_forces/pallas_call | solution.py:220
  98.6 58.6 %return_forces.1 = f32[6,2,8,32,128]{4,3,2,1,0:T(8,128)S(1)} custom-call(f32[4,3,2,8,32,128]{5,4,3,2,1,0:T(8,128)S(1)} %bitcast.24, f32[4,3,2,8,32,128]{5,4,3,2,1,0:T(8,128)S(1)} %bitcast.25), custom_call_target="tpu_custom_call" | custom-call | tf_op jit(solution)/shard_map/return_forces/pallas_call | solution.py:576
  157.2 0.8 collective-permute-start.2
  158.0 0.1 slice.20
  158.1 13.6 %collective-permute-done.2 = f32[4,8,32,128]{3,2,1,0:T(8,128)S(1)} collective-permute-done((f32[4,8,32,128]{3,2,1,0:T(8,128)S(1)}, f32[4,8,32,128]{3,2,1,0:T(8,128)S(1)}, u32[]{:S(2)}, u32[]{:S(2)}) %collective-permute-start.2) | collective-permute-done | bytes 524320 | tf_op jit(solution)/shard_map/ppermute | solution.py:596
  171.8 1.6 multiply_add_fusion
  (1 shorter events, 0.0 us)
Async XLA Ops:
  2.5 66.5 %collective-permute-start.1 = (f32[8,2,32,128]{3,2,1,0:T(8,128)}, f32[8,2,32,128]{3,2,1,0:T(8,128)S(1)}, u32[]{:S(2)}, u32[]{:S(2)}) collective-permute-start(f32[8,2,32,128]{3,2,1,0:T(8,128)} %get-tuple-element.16), channel_id=1, source_target_pairs={{1,0},{2,1},{3,2},{4,3},{5,4},{6,5},{7,6},{9,8},{10,9},{11,10},{12... | collective-permute-start | bytes 786440 | tf_op jit(solution)/shard_map/ppermute | solution.py:608
  4.4 64.6 %collective-permute-start = (f32[8,2,32,128]{3,2,1,0:T(8,128)}, f32[8,2,32,128]{3,2,1,0:T(8,128)}, u32[]{:S(2)}, u32[]{:S(2)}) collective-permute-start(f32[8,2,32,128]{3,2,1,0:T(8,128)} %get-tuple-element.17), channel_id=1, source_target_pairs={{0,1},{1,2},{2,3},{3,4},{4,5},{5,6},{6,7},{8,9},{9,10},{10,11},{11... | collective-permute-start | bytes 786440 | tf_op jit(solution)/shard_map/ppermute | solution.py:607
  7.5 1.2 copy-start
  65.7 2.7 %copy-start.2 = (f32[4,6,2,8,32,128]{5,4,3,2,1,0:T(8,128)}, f32[4,6,2,8,32,128]{5,4,3,2,1,0:T(8,128)S(1)}, u32[]{:S(2)}) copy-start(f32[4,6,2,8,32,128]{5,4,3,2,1,0:T(8,128)S(1)} %get-tuple-element.10) | copy-start | bytes 18874372
  69.0 1.2 copy-start.1
  70.3 1.2 copy-start.4
  71.5 1.2 copy-start.5
  77.1 2.8 %copy-start.3 = (f32[4,6,2,8,32,128]{5,4,3,2,1,0:T(8,128)S(1)}, f32[4,6,2,8,32,128]{5,4,3,2,1,0:T(8,128)}, u32[]{:S(2)}) copy-start(f32[4,6,2,8,32,128]{5,4,3,2,1,0:T(8,128)} %copy-done.2) | copy-start | bytes 18874372
  157.2 14.5 %collective-permute-start.2 = (f32[4,8,32,128]{3,2,1,0:T(8,128)S(1)}, f32[4,8,32,128]{3,2,1,0:T(8,128)S(1)}, u32[]{:S(2)}, u32[]{:S(2)}) collective-permute-start(f32[4,8,32,128]{3,2,1,0:T(8,128)S(1)} %bitcast.31), channel_id=1, source_target_pairs={{0,8},{8,16},{16,24},{24,0},{1,9},{9,17},{17,25},{25,1},{2,10},{10... | collective-permute-start | bytes 1572872 | tf_op jit(solution)/shard_map/ppermute | solution.py:596
